TPU v7x, 256 devices: a whole 4x4x8 slice. The times are simulated.
256 devices in a mesh: rep: 2 (over z_lo), lev: 4 (over z_hi), tile: 32 (over y, x, core).
Axes of the slice: x: 4, y: 4, z: 8 (z_hi: 4, z_lo: 2; z = z_hi * 2 + z_lo), core: 2. Of those that a mesh axis runs over, the one named last changes fastest.
Arguments:
- tokens: bfloat16 [2, 8, 32, 8, 8, 768], P('rep', 'lev', 'tile'), may hold values from -6 to 6
- w_qkv: bfloat16 [768, 2304], P('tile'), may hold values from -0.21875 to 0.21875
- w_proj: bfloat16 [768, 768], P('tile'), may hold values from -0.21875 to 0.21875
- seam_codes: int32 [32, 2], replicated, may hold values from 0 to 1
- upstream: bfloat16 [2, 8, 32, 8, 8, 768], P('rep', 'lev', 'tile'), may hold values from -6 to 6
Outputs:
- output: bfloat16 [2, 8, 32, 8, 8, 768], P('rep', 'lev', 'tile')
- grad_tokens: bfloat16 [2, 8, 32, 8, 8, 768], P('rep', 'lev', 'tile')
- grad_qkv: float32 [768, 2304], P('tile')
- grad_proj: float32 [768, 768], P('tile')
Inputs may be any that keep to these rules, and one draw needn't show every extreme that they name: The tiles form a periodic grid of four rows of 8 tiles: tile t's eastern neighbour is (t + 1) mod 32 and its northern neighbour (t + 8) mod 32. seam_codes[t, 0] is 1 where the seam to the eastern neighbour runs reversed, seam_codes[t, 1] likewise for the northern neighbour.
All inputs are finite; a program needn't handle non-finite values.
Results may differ from a plain program's by a relative error of at most 0.019.
Values may be sent and summed in bfloat16 or wider, within the bound.
A program may use at most 64 MiB of HBM per device.

v0:
```python
import jax
import jax.numpy as jnp
from jax import lax
from jax.sharding import PartitionSpec as P

HEAD_DIM = 32
WIN = 8
WIN_LEV = 2


EPSILON = 1e-05


def shifted(value, axis, steps):
    count = lax.axis_size(axis)
    pairs = [(source, (source + steps) % count) for source in range(count)]
    return lax.ppermute(value, axis, pairs)


def sent_together(arrays, axis, dim, along):
    both = jnp.concatenate(arrays, axis=along)
    out, at, gathered = (lax.all_gather(both, axis, axis=dim, tiled=True), 0, [])
    for a in arrays:
        gathered.append(lax.slice_in_dim(out, at, at + a.shape[along], axis=along))
        at += a.shape[along]
    return tuple(gathered)


def cut_along(array, dim, peers):
    dims = array.shape
    blocks = array.reshape(*dims[:dim], peers, dims[dim] // peers, *dims[dim + 1 :])
    return jnp.moveaxis(blocks, dim, 0)


def sum_at_owner(array, axis, dim):
    blocks = cut_along(array, dim, lax.axis_size(axis))
    arrived = lax.all_to_all(blocks, axis, split_axis=0, concat_axis=0, tiled=True)
    return arrived.astype(jnp.float32).sum(axis=0)


def from_everyone(array, axis):
    peers = lax.axis_size(axis)
    return lax.all_to_all(
        jnp.broadcast_to(array[None], (peers, *array.shape)), axis, 0, 0, tiled=True
    )


def of_everyone(array, axis):
    everything = from_everyone(array, axis)
    return jnp.sum(everything.astype(jnp.float32), axis=0)


def layer_stats(token_rows):
    values = token_rows.astype(jnp.float32)
    center = jnp.mean(values, axis=1, keepdims=True)
    spread = jnp.mean(jnp.square(values - center), axis=1, keepdims=True)
    inverse = lax.rsqrt(spread + EPSILON)
    return ((values - center) * inverse, inverse)


def norm_backward(upstream_rows, grad_hidden, normalized, inverse):
    centre = jnp.mean(grad_hidden, axis=1, keepdims=True)
    projected = jnp.mean(grad_hidden * normalized, axis=1, keepdims=True)
    total_grad = (
        upstream_rows.astype(jnp.float32)
        + (grad_hidden - centre - normalized * projected) * inverse
    )
    return total_grad.astype(jnp.bfloat16)


def roll_local(grid_field, east_flag, north_flag, north_step):
    shift_cells = WIN // 2
    east_part = shifted(grid_field[:, :, :shift_cells], "tile", -1)
    east_part = jnp.where(east_flag, east_part[:, ::-1], east_part)
    across = jnp.concatenate([grid_field[:, :, shift_cells:], east_part], axis=2)
    north_part = shifted(across[:, :shift_cells], "tile", -north_step)
    north_part = jnp.where(north_flag, north_part[:, :, ::-1], north_part)
    upward = jnp.concatenate([across[:, shift_cells:], north_part], axis=1)
    level_part = shifted(upward[:1], "lev", -1)
    return jnp.concatenate([upward[1:], level_part], axis=0)


def unroll_local(rolled, east_flag, north_flag, north_step):
    shift_cells = WIN // 2
    extent = rolled.shape[1]
    level_part = shifted(rolled[-1:], "lev", 1)
    upward = jnp.concatenate([level_part, rolled[:-1]], axis=0)
    north_part = upward[:, extent - shift_cells :]
    north_part = jnp.where(north_flag, north_part[:, :, ::-1], north_part)
    north_part = shifted(north_part, "tile", north_step)
    across = jnp.concatenate([north_part, upward[:, : extent - shift_cells]], axis=1)
    east_part = across[:, :, extent - shift_cells :]
    east_part = jnp.where(east_flag, east_part[:, ::-1], east_part)
    east_part = shifted(east_part, "tile", 1)
    return jnp.concatenate([east_part, across[:, :, : extent - shift_cells]], axis=2)


def to_windows(grid_field):
    levels = grid_field.shape[0]
    extent = grid_field.shape[1]
    channels = grid_field.shape[3]
    blocks = grid_field.reshape(
        levels // WIN_LEV, WIN_LEV, extent // WIN, WIN, extent // WIN, WIN, channels
    )
    blocks = blocks.transpose(0, 2, 4, 1, 3, 5, 6)
    return blocks.reshape(-1, WIN_LEV * WIN * WIN, channels)


def from_windows(windows, levels, extent):
    channels = windows.shape[-1]
    blocks = windows.reshape(
        levels // WIN_LEV, extent // WIN, extent // WIN, WIN_LEV, WIN, WIN, channels
    )
    blocks = blocks.transpose(0, 3, 1, 4, 2, 5, 6)
    return blocks.reshape(levels, extent, extent, channels)


def split_heads(packed):
    windows = packed.shape[0]
    tokens = packed.shape[1]
    model_width = packed.shape[2] // 3
    head_count = model_width // HEAD_DIM
    query_part = packed[:, :, :model_width].reshape(windows, tokens, head_count, HEAD_DIM)
    key_part = packed[:, :, model_width : 2 * model_width].reshape(
        windows, tokens, head_count, HEAD_DIM
    )
    value_part = packed[:, :, 2 * model_width :].reshape(windows, tokens, head_count, HEAD_DIM)
    return (query_part, key_part, value_part)


def window_mask(wrap_flags, tokens):
    level_of = jnp.arange(tokens, dtype=jnp.int32) // (WIN * WIN)
    same_level = level_of[:, None] == level_of[None, :]
    allowed = jnp.logical_or(
        same_level[None, None], jnp.logical_not(wrap_flags)[:, None, None, None]
    )
    return allowed.astype(jnp.float32)


def attend_forward(packed, wrap_flags):
    query_part, key_part, value_part = split_heads(packed)
    scores = jnp.einsum(
        "wqhd,wkhd->whqk", query_part, key_part, preferred_element_type=jnp.float32
    ) * HEAD_DIM ** (-0.5)
    raised = jnp.exp(scores) * window_mask(wrap_flags, packed.shape[1])
    prob = raised / jnp.sum(raised, axis=-1, keepdims=True)
    prob_low = prob.astype(jnp.bfloat16)
    attended = jnp.einsum(
        "whqk,wkhd->wqhd", prob_low, value_part, preferred_element_type=jnp.float32
    )
    attended = attended.astype(jnp.bfloat16).reshape(packed.shape[0], packed.shape[1], -1)
    return (attended, prob, prob_low)


def attend_backward(packed, back_windows, prob, prob_low):
    query_part, key_part, value_part = split_heads(packed)
    back_heads = back_windows.reshape(query_part.shape)
    grad_value = jnp.einsum(
        "whqk,wqhd->wkhd", prob_low, back_heads, preferred_element_type=jnp.float32
    )
    grad_prob = jnp.einsum(
        "wqhd,wkhd->whqk", back_heads, value_part, preferred_element_type=jnp.float32
    )
    centre = jnp.sum(prob * grad_prob, axis=-1, keepdims=True)
    grad_scores = (prob * (grad_prob - centre) * HEAD_DIM ** (-0.5)).astype(jnp.bfloat16)
    grad_query = jnp.einsum(
        "whqk,wkhd->wqhd", grad_scores, key_part, preferred_element_type=jnp.float32
    )
    grad_key = jnp.einsum(
        "whqk,wqhd->wkhd", grad_scores, query_part, preferred_element_type=jnp.float32
    )
    windows = packed.shape[0]
    tokens = packed.shape[1]
    joined = jnp.concatenate(
        [
            grad_query.reshape(windows, tokens, -1),
            grad_key.reshape(windows, tokens, -1),
            grad_value.reshape(windows, tokens, -1),
        ],
        axis=-1,
    )
    return joined.astype(jnp.bfloat16)


def shards(tokens, w_qkv, w_proj, seam_codes, upstream):
    levels = tokens.shape[1]
    extent = tokens.shape[3]
    model_width = tokens.shape[5]
    tiles_count = lax.axis_size("tile")
    north_step = tiles_count // 4
    tile_here = lax.axis_index("tile")
    east_flag = seam_codes[tile_here, 0] == 1
    north_flag = seam_codes[tile_here, 1] == 1
    top_level = lax.axis_index("lev") == lax.axis_size("lev") - 1
    per_level = extent // WIN * (extent // WIN)
    window_total = levels // WIN_LEV * per_level
    lev_window = jnp.arange(window_total, dtype=jnp.int32) // per_level
    wrap_flags = jnp.logical_and(top_level, lev_window == levels // WIN_LEV - 1)
    contract_last = (((1,), (1,)), ((), ()))
    contract_first = (((0,), (0,)), ((), ()))
    grid_in = tokens.reshape(levels, extent, extent, model_width)
    grid_up = upstream.reshape(levels, extent, extent, model_width)
    paired = roll_local(
        jnp.concatenate([grid_in, grid_up], axis=-1), east_flag, north_flag, north_step
    )
    grid_in = paired[..., :model_width]
    grid_up = paired[..., model_width:]
    token_rows = grid_in.reshape(-1, model_width)
    upstream_rows = grid_up.reshape(-1, model_width)
    normalized, inverse = layer_stats(token_rows)
    hidden = normalized.astype(jnp.bfloat16)
    full_qkv, full_proj = sent_together((w_qkv, w_proj), "tile", 0, 1)
    projected = jnp.dot(hidden, full_qkv, preferred_element_type=jnp.float32).astype(jnp.bfloat16)
    grid_qkv = projected.reshape(levels, extent, extent, 3 * model_width)
    windows_qkv = to_windows(grid_qkv)
    attended, prob, prob_low = attend_forward(windows_qkv, wrap_flags)
    grid_mixed = from_windows(attended, levels, extent)
    mixed_in = grid_mixed.reshape(-1, model_width)
    mixed_out = lax.dot_general(
        mixed_in, full_proj, contract_last, preferred_element_type=jnp.float32
    )
    back_mix = jnp.dot(upstream_rows, full_proj, preferred_element_type=jnp.float32)
    output_low = (token_rows.astype(jnp.float32) + mixed_out).astype(jnp.bfloat16)
    back_low = back_mix.astype(jnp.bfloat16)
    grid_back = back_low.reshape(levels, extent, extent, model_width)
    grad_windows = attend_backward(windows_qkv, to_windows(grid_back), prob, prob_low)
    grid_grad = from_windows(grad_windows, levels, extent)
    grad_qkv_tok = grid_grad.reshape(-1, 3 * model_width)
    grad_hidden = lax.dot_general(
        grad_qkv_tok, full_qkv, contract_last, preferred_element_type=jnp.float32
    )
    grad_low = norm_backward(upstream_rows, grad_hidden, normalized, inverse)
    grid_output = output_low.reshape(levels, extent, extent, model_width)
    grid_dx = grad_low.reshape(levels, extent, extent, model_width)
    paired = unroll_local(
        jnp.concatenate([grid_output, grid_dx], axis=-1), east_flag, north_flag, north_step
    )
    grid_output = paired[..., :model_width]
    grid_dx = paired[..., model_width:]
    columns = hidden
    share_qkv = lax.psum_scatter(
        lax.dot_general(
            columns, grad_qkv_tok, contract_first, preferred_element_type=jnp.float32
        ).astype(jnp.bfloat16),
        "tile",
        scatter_dimension=0,
        tiled=True,
    )
    columns = upstream_rows
    share_proj = sum_at_owner(
        lax.dot_general(
            columns, mixed_in, contract_first, preferred_element_type=jnp.float32
        ).astype(jnp.bfloat16),
        "tile",
        0,
    )
    grad_qkv, grad_proj = (
        of_everyone(share_qkv, ("rep", "lev")).astype(jnp.float32),
        of_everyone(share_proj.astype(jnp.bfloat16), ("rep", "lev")).astype(jnp.float32),
    )
    return (grid_output.reshape(tokens.shape), grid_dx.reshape(tokens.shape), grad_qkv, grad_proj)


def solution(mesh):
    in_specs = (
        P("rep", "lev", "tile", None, None, None),
        P("tile", None),
        P("tile", None),
        P(),
        P("rep", "lev", "tile", None, None, None),
    )
    out_specs = (
        P("rep", "lev", "tile", None, None, None),
        P("rep", "lev", "tile", None, None, None),
        P("tile", None),
        P("tile", None),
    )
    return jax.shard_map(shards, mesh=mesh, in_specs=in_specs, out_specs=out_specs, check_vma=False)
```

profile of v0, /device:TPU:1, one launch (start us, length us, event | category | flops | bytes accessed | tf_op | source)
XLA Modules:
  0.0 211.9 jit_solution(17315963661645362018)
XLA Ops:
  7.2 0.0 all-gather.2.cloned.1.call-start
  7.2 1.6 pad_maximum_fusion.9
  8.8 0.0 all-gather.2.cloned.1.call-update
  8.8 0.0 reduce-scatter.2.cloned.1.call-start
  8.9 1.4 fusion.38
  10.3 3.3 %collective-permute-start = (bf16[2,8,4,1536]{3,2,1,0:T(4,128)(2,1)S(1)}, bf16[2,8,4,1536]{3,2,1,0:T(4,128)(2,1)S(1)}, u32[]{:S(2)}, u32[]{:S(2)}) collective-permute-start(bf16[2,8,4,1536]{3,2,1,0:T(4,128)(2,1)S(1)} %get-tuple-element.20), channel_id=1, source_target_pairs={{0,31},{1,0},{2,1},{3,2},{4,3},{5,4},{6,5},{7,6},{8,7},{9,8},{10,9... | collective-permute-start | bytes 589832 | tf_op jit(solution)/shard_map/ppermute | solution.py:17
  13.6 1.3 constant_dynamic-slice_fusion
  15.6 0.7 collective-permute-done
  16.3 0.1 reverse_select_fusion.1
  16.4 0.2 fusion.37
  16.6 2.8 %collective-permute-start.1 = (bf16[2,4,8,1536]{3,2,1,0:T(8,128)(2,1)S(1)}, bf16[2,4,8,1536]{3,2,1,0:T(8,128)(2,1)S(1)}, u32[]{:S(2)}, u32[]{:S(2)}) collective-permute-start(bf16[2,4,8,1536]{3,2,1,0:T(8,128)(2,1)S(1)} %get-tuple-element.18), channel_id=1, source_target_pairs={{0,24},{1,25},{2,26},{3,27},{4,28},{5,29},{6,30},{7,31},{8,0},{9,1... | collective-permute-start | bytes 589832 | tf_op jit(solution)/shard_map/ppermute | solution.py:17
  20.1 2.4 %collective-permute-done.1 = bf16[2,4,8,1536]{3,2,1,0:T(8,128)(2,1)S(1)} collective-permute-done((bf16[2,4,8,1536]{3,2,1,0:T(8,128)(2,1)S(1)}, bf16[2,4,8,1536]{3,2,1,0:T(8,128)(2,1)S(1)}, u32[]{:S(2)}, u32[]{:S(2)}) %collective-permute-start.1) | collective-permute-done | bytes 196640 | tf_op jit(solution)/shard_map/ppermute | solution.py:17
  22.5 0.3 rev.13
  22.9 6.1 %collective-permute-start.2 = (bf16[1,8,8,1536]{3,2,1,0:T(8,128)(2,1)S(1)}, bf16[1,8,8,1536]{3,2,1,0:T(8,128)(2,1)S(1)}, u32[]{:S(2)}, u32[]{:S(2)}) collective-permute-start(bf16[1,8,8,1536]{3,2,1,0:T(8,128)(2,1)S(1)} %get-tuple-element.16), channel_id=1, source_target_pairs={{0,96},{32,0},{64,32},{96,64},{1,97},{33,1},{65,33},{97,65},{2,98}... | collective-permute-start | bytes 589832 | tf_op jit(solution)/shard_map/ppermute | solution.py:17
  29.0 0.1 or_convert_fusion
  29.1 4.0 %collective-permute-done.2 = bf16[1,8,8,1536]{3,2,1,0:T(8,128)(2,1)S(1)} collective-permute-done((bf16[1,8,8,1536]{3,2,1,0:T(8,128)(2,1)S(1)}, bf16[1,8,8,1536]{3,2,1,0:T(8,128)(2,1)S(1)}, u32[]{:S(2)}, u32[]{:S(2)}) %collective-permute-start.2) | collective-permute-done | bytes 196640 | tf_op jit(solution)/shard_map/ppermute | solution.py:17
  33.1 0.1 convert_reduce_fusion.2
  33.2 0.1 div.36
  33.3 0.2 multiply_reduce_fusion.2
  33.5 0.1 rsqrt.12
  33.6 0.1 fusion.32
  33.8 33.6 %all-gather.2.cloned.1.call-done = bf16[768,3072]{1,0:T(8,128)(2,1)} async-done(((bf16[24,3072]{1,0:T(8,128)(2,1)}), bf16[768,3072]{1,0:T(8,128)(2,1)}) %all-gather.2.cloned.1.call-update) | async-done | bytes 4718608 | tf_op jit(solution)/shard_map/all_gather | solution.py:22
  67.4 2.6 %fusion.1 = bf16[1,128,2304]{2,1,0:T(8,128)(2,1)S(1)} fusion(bf16[128,768]{1,0:T(8,128)(2,1)S(1)} %fusion.32, bf16[768,3072]{1,0:T(8,128)(2,1)} %all-gather.2.cloned.1.call-done), kind=kOutput, calls=%fused_computation.3 | convolution fusion | flops 453279744 | bytes 4325376 | tf_op jit(solution)/shard_map/dot_general | solution.py:213
  70.1 0.2 copy.31
  70.2 0.2 copy.30
  70.4 1.8 fusion.24
  72.2 0.5 exponential_multiply_fusion
  72.7 1.6 convolution_convert_fusion.3
  74.3 0.8 copy.33
  75.1 0.8 copy.29
  75.9 1.4 fusion.51
  77.4 3.1 %fusion.14 = bf16[24,32,128]{2,1,0:T(8,128)(2,1)} fusion(bf16[128,24,32]{0,2,1:T(8,128)(2,1)} %bitcast.79, f32[24,128,128]{1,2,0:T(8,128)} %fusion.24, f32[24,128,128]{1,2,0:T(8,128)S(1)} %fusion.51), kind=kOutput, calls=%fused_computation.16 | convolution fusion | flops 27233408 | bytes 3538944 | tf_op jit(solution)/shard_map/whqk,wkhd->wqhd/dot_general | solution.py:166
  80.4 3.2 %fusion.17 = bf16[24,32,128]{2,1,0:T(8,128)(2,1)} fusion(bf16[128,24,32]{0,2,1:T(8,128)(2,1)} %bitcast.82, f32[24,128,128]{1,2,0:T(8,128)} %fusion.24, f32[24,128,128]{1,2,0:T(8,128)S(1)} %fusion.51), kind=kOutput, calls=%fused_computation.17 | convolution fusion | flops 27233408 | bytes 3538944 | tf_op jit(solution)/shard_map/whqk,wqhd->wkhd/dot_general | solution.py:169
  83.6 1.5 convolution_convert_fusion.4
  85.2 2.9 %convolution_convert_fusion = bf16[768,2304]{1,0:T(8,128)(2,1)} fusion(bf16[128,768]{1,0:T(8,128)(2,1)S(1)} %copy-done.1, bf16[128,768]{0,1:T(8,128)(2,1)S(1)} %bitcast.93, bf16[128,768]{0,1:T(8,128)(2,1)S(1)} %bitcast.91, bf16[128,768]{0,1:T(8,128)(2,1)S(1)} %bitcast.89), kind=kOutput, calls=%fused_computation.1 | convolution fusion | flops 456523776 | bytes 4325376 | tf_op jit(solution)/shard_map/dot_general | solution.py:242
  88.1 0.0 reduce-scatter.2.cloned.1.call-update
  88.1 0.9 copy-done.2
  89.0 0.3 convolution_convert_fusion.5
  89.3 1.6 convolution_convert_fusion.2
  90.9 5.1 %all-to-all-start.1 = ((bf16[32,24,768]{2,1,0:T(8,128)(2,1)}), bf16[32,24,768]{2,1,0:T(8,128)(2,1)S(1)}, u32[]{:S(2)}, u32[]{:S(2)}) async-start(bf16[32,24,768]{2,1,0:T(8,128)(2,1)} %bitcast.29), calls=%async_computation.2 | async-start | bytes 2359296 | tf_op jit(solution)/shard_map/all_to_all | solution.py:37
  96.1 3.4 %fusion.48 = (f32[128]{0:T(128)S(1)}, f32[128]{0:T(128)S(1)}, f32[128,768]{1,0:T(8,128)S(1)}) fusion(f32[128]{0:T(128)S(1)} %rsqrt.12, f32[128]{0:T(128)S(1)} %div.36, bf16[2,8,8,768]{3,2,1,0:T(8,128)(2,1)S(1)} %get-tuple-element.7, bf16[768,3072]{1,0:T(8,128)(2,1)} %all-gather.2.cloned.1.call-done, bf16[128,768]{0,1:T(8,128)(2,1)S(1)} %bitcast.94, ...), kind=kOutput, calls=%fused_computation.92 | convolution fusion | flops 455343872 | bytes 4720640 | tf_op jit(solution)/shard_map/dot_general | solution.py:229
  99.5 0.2 add_convert_fusion
  99.7 1.8 fusion.20
  101.6 2.5 %collective-permute-start.3 = (bf16[1,8,8,1536]{3,2,1,0:T(8,128)(2,1)S(1)}, bf16[1,8,8,1536]{3,2,1,0:T(8,128)(2,1)S(1)}, u32[]{:S(2)}, u32[]{:S(2)}) collective-permute-start(bf16[1,8,8,1536]{3,2,1,0:T(8,128)(2,1)S(1)} %fusion.34), channel_id=1, source_target_pairs={{0,32},{32,64},{64,96},{96,0},{1,33},{33,65},{65,97},{97,1},{2,34}... | collective-permute-start | bytes 589832 | tf_op jit(solution)/shard_map/ppermute | solution.py:17
  104.1 8.7 %collective-permute-done.3 = bf16[1,8,8,1536]{3,2,1,0:T(8,128)(2,1)S(1)} collective-permute-done((bf16[1,8,8,1536]{3,2,1,0:T(8,128)(2,1)S(1)}, bf16[1,8,8,1536]{3,2,1,0:T(8,128)(2,1)S(1)}, u32[]{:S(2)}, u32[]{:S(2)}) %collective-permute-start.3) | collective-permute-done | bytes 196640 | tf_op jit(solution)/shard_map/ppermute | solution.py:17
  112.9 0.3 rev.14
  113.2 0.6 all-to-all-done.1
  113.8 0.2 reduce_sum.91
  114.0 0.7 broadcast_in_dim.5
  114.7 7.8 %all-to-all-start.2 = ((bf16[8,24,768]{2,1,0:T(8,128)(2,1)}), bf16[8,24,768]{2,1,0:T(8,128)(2,1)S(1)}, u32[]{:S(2)}, u32[]{:S(2)}) async-start(bf16[8,24,768]{2,1,0:T(8,128)(2,1)} %broadcast_in_dim.5), calls=%async_computation.3 | async-start | bytes 589824 | tf_op jit(solution)/shard_map/all_to_all | solution.py:43
  122.5 1.3 collective-permute-start.4
  123.8 6.5 %all-to-all-done.2 = bf16[8,24,768]{2,1,0:T(8,128)(2,1)S(1)} async-done(((bf16[8,24,768]{2,1,0:T(8,128)(2,1)}), bf16[8,24,768]{2,1,0:T(8,128)(2,1)S(1)}, u32[]{:S(2)}, u32[]{:S(2)}) %all-to-all-start.2) | async-done | bytes 294944 | tf_op jit(solution)/shard_map/all_to_all | solution.py:43
  130.3 43.4 %reduce-scatter.2.cloned.1.call-done = bf16[24,2304]{1,0:T(8,128)(2,1)} async-done(((bf16[768,2304]{1,0:T(8,128)(2,1)}), bf16[24,2304]{1,0:T(8,128)(2,1)}) %reduce-scatter.2.cloned.1.call-update) | async-done | bytes 110608 | tf_op jit(solution)/shard_map/reduce_scatter | solution.py:241
  173.6 1.9 broadcast_in_dim.4
  175.5 6.7 %all-to-all-start = ((bf16[8,24,2304]{2,1,0:T(8,128)(2,1)}), bf16[8,24,2304]{2,1,0:T(8,128)(2,1)S(1)}, u32[]{:S(2)}, u32[]{:S(2)}) async-start(bf16[8,24,2304]{2,1,0:T(8,128)(2,1)} %broadcast_in_dim.4), calls=%async_computation.1 | async-start | bytes 1769472 | tf_op jit(solution)/shard_map/all_to_all | solution.py:43
  182.3 0.2 fusion.33
  182.4 0.1 reverse_select_fusion
  182.5 3.4 %collective-permute-start.5 = (bf16[2,8,4,1536]{3,2,1,0:T(4,128)(2,1)S(1)}, bf16[2,8,4,1536]{3,2,1,0:T(4,128)(2,1)S(1)}, u32[]{:S(2)}, u32[]{:S(2)}) collective-permute-start(bf16[2,8,4,1536]{3,2,1,0:T(4,128)(2,1)S(1)} %reverse_select_fusion), channel_id=1, source_target_pairs={{0,1},{1,2},{2,3},{3,4},{4,5},{5,6},{6,7},{7,8},{8,9},{9,10},{10,1... | collective-permute-start | bytes 589832 | tf_op jit(solution)/shard_map/ppermute | solution.py:17
  186.0 2.6 %collective-permute-done.5 = bf16[2,8,4,1536]{3,2,1,0:T(4,128)(2,1)S(1)} collective-permute-done((bf16[2,8,4,1536]{3,2,1,0:T(4,128)(2,1)S(1)}, bf16[2,8,4,1536]{3,2,1,0:T(4,128)(2,1)S(1)}, u32[]{:S(2)}, u32[]{:S(2)}) %collective-permute-start.5) | collective-permute-done | bytes 196640 | tf_op jit(solution)/shard_map/ppermute | solution.py:17
  188.6 0.2 fusion.27
  188.7 0.8 slice_bitcast_fusion
  189.5 0.7 convert_reduce_fusion.1
  190.2 14.1 %all-to-all-done = bf16[8,24,2304]{2,1,0:T(8,128)(2,1)S(1)} async-done(((bf16[8,24,2304]{2,1,0:T(8,128)(2,1)}), bf16[8,24,2304]{2,1,0:T(8,128)(2,1)S(1)}, u32[]{:S(2)}, u32[]{:S(2)}) %all-to-all-start) | async-done | bytes 884768 | tf_op jit(solution)/shard_map/all_to_all | solution.py:43
  204.3 0.8 convert_reduce_fusion
  (26 shorter events, 0.3 us)
Async XLA Ops:
  7.2 60.2 %all-gather.2.cloned.1.call-start = ((), (), s32[]{:S(2)}) async-start(), calls=%async_computation.4 | async-start | bytes 4866048 | tf_op jit(solution)/shard_map/all_gather | solution.py:22
  8.8 164.8 %reduce-scatter.2.cloned.1.call-start = ((), (), s32[]{:S(2)}) async-start(), calls=%async_computation.5 | async-start | bytes 3649536 | tf_op jit(solution)/shard_map/reduce_scatter | solution.py:241
  10.3 6.0 %collective-permute-start = (bf16[2,8,4,1536]{3,2,1,0:T(4,128)(2,1)S(1)}, bf16[2,8,4,1536]{3,2,1,0:T(4,128)(2,1)S(1)}, u32[]{:S(2)}, u32[]{:S(2)}) collective-permute-start(bf16[2,8,4,1536]{3,2,1,0:T(4,128)(2,1)S(1)} %get-tuple-element.20), channel_id=1, source_target_pairs={{0,31},{1,0},{2,1},{3,2},{4,3},{5,4},{6,5},{7,6},{8,7},{9,8},{10,9... | collective-permute-start | bytes 589832 | tf_op jit(solution)/shard_map/ppermute | solution.py:17
  16.6 5.9 %collective-permute-start.1 = (bf16[2,4,8,1536]{3,2,1,0:T(8,128)(2,1)S(1)}, bf16[2,4,8,1536]{3,2,1,0:T(8,128)(2,1)S(1)}, u32[]{:S(2)}, u32[]{:S(2)}) collective-permute-start(bf16[2,4,8,1536]{3,2,1,0:T(8,128)(2,1)S(1)} %get-tuple-element.18), channel_id=1, source_target_pairs={{0,24},{1,25},{2,26},{3,27},{4,28},{5,29},{6,30},{7,31},{8,0},{9,1... | collective-permute-start | bytes 589832 | tf_op jit(solution)/shard_map/ppermute | solution.py:17
  22.9 10.2 %collective-permute-start.2 = (bf16[1,8,8,1536]{3,2,1,0:T(8,128)(2,1)S(1)}, bf16[1,8,8,1536]{3,2,1,0:T(8,128)(2,1)S(1)}, u32[]{:S(2)}, u32[]{:S(2)}) collective-permute-start(bf16[1,8,8,1536]{3,2,1,0:T(8,128)(2,1)S(1)} %get-tuple-element.16), channel_id=1, source_target_pairs={{0,96},{32,0},{64,32},{96,64},{1,97},{33,1},{65,33},{97,65},{2,98}... | collective-permute-start | bytes 589832 | tf_op jit(solution)/shard_map/ppermute | solution.py:17
  33.7 36.3 %copy-start = (bf16[128,768]{1,0:T(8,128)(2,1)}, bf16[128,768]{1,0:T(8,128)(2,1)S(1)}, u32[]{:S(2)}) copy-start(bf16[128,768]{1,0:T(8,128)(2,1)S(1)} %fusion.32) | copy-start | bytes 589828
  70.2 2.0 copy-start.3
  70.4 1.8 copy-start.4
  83.6 1.5 copy-start.1
  83.6 1.5 copy-start.5
  83.6 1.6 copy-start.6
  88.1 0.9 copy-start.2
  90.9 22.8 %all-to-all-start.1 = ((bf16[32,24,768]{2,1,0:T(8,128)(2,1)}), bf16[32,24,768]{2,1,0:T(8,128)(2,1)S(1)}, u32[]{:S(2)}, u32[]{:S(2)}) async-start(bf16[32,24,768]{2,1,0:T(8,128)(2,1)} %bitcast.29), calls=%async_computation.2 | async-start | bytes 2359296 | tf_op jit(solution)/shard_map/all_to_all | solution.py:37
  101.6 11.2 %collective-permute-start.3 = (bf16[1,8,8,1536]{3,2,1,0:T(8,128)(2,1)S(1)}, bf16[1,8,8,1536]{3,2,1,0:T(8,128)(2,1)S(1)}, u32[]{:S(2)}, u32[]{:S(2)}) collective-permute-start(bf16[1,8,8,1536]{3,2,1,0:T(8,128)(2,1)S(1)} %fusion.34), channel_id=1, source_target_pairs={{0,32},{32,64},{64,96},{96,0},{1,33},{33,65},{65,97},{97,1},{2,34}... | collective-permute-start | bytes 589832 | tf_op jit(solution)/shard_map/ppermute | solution.py:17
  114.7 15.6 %all-to-all-start.2 = ((bf16[8,24,768]{2,1,0:T(8,128)(2,1)}), bf16[8,24,768]{2,1,0:T(8,128)(2,1)S(1)}, u32[]{:S(2)}, u32[]{:S(2)}) async-start(bf16[8,24,768]{2,1,0:T(8,128)(2,1)} %broadcast_in_dim.5), calls=%async_computation.3 | async-start | bytes 589824 | tf_op jit(solution)/shard_map/all_to_all | solution.py:43
  122.5 59.8 %collective-permute-start.4 = (bf16[2,4,8,1536]{3,2,1,0:T(8,128)(2,1)S(1)}, bf16[2,4,8,1536]{3,2,1,0:T(8,128)(2,1)S(1)}, u32[]{:S(2)}, u32[]{:S(2)}) collective-permute-start(bf16[2,4,8,1536]{3,2,1,0:T(8,128)(2,1)S(1)} %get-tuple-element.13), channel_id=1, source_target_pairs={{0,8},{1,9},{2,10},{3,11},{4,12},{5,13},{6,14},{7,15},{8,16},{9,17... | collective-permute-start | bytes 589832 | tf_op jit(solution)/shard_map/ppermute | solution.py:17
  175.5 28.8 %all-to-all-start = ((bf16[8,24,2304]{2,1,0:T(8,128)(2,1)}), bf16[8,24,2304]{2,1,0:T(8,128)(2,1)S(1)}, u32[]{:S(2)}, u32[]{:S(2)}) async-start(bf16[8,24,2304]{2,1,0:T(8,128)(2,1)} %broadcast_in_dim.4), calls=%async_computation.1 | async-start | bytes 1769472 | tf_op jit(solution)/shard_map/all_to_all | solution.py:43
  182.5 6.0 %collective-permute-start.5 = (bf16[2,8,4,1536]{3,2,1,0:T(4,128)(2,1)S(1)}, bf16[2,8,4,1536]{3,2,1,0:T(4,128)(2,1)S(1)}, u32[]{:S(2)}, u32[]{:S(2)}) collective-permute-start(bf16[2,8,4,1536]{3,2,1,0:T(4,128)(2,1)S(1)} %reverse_select_fusion), channel_id=1, source_target_pairs={{0,1},{1,2},{2,3},{3,4},{4,5},{5,6},{6,7},{7,8},{8,9},{9,10},{10,1... | collective-permute-start | bytes 589832 | tf_op jit(solution)/shard_map/ppermute | solution.py:17
Sparse Core Ops, SparseCore 0:
  11.1 56.1 all-gather.1
  88.2 85.3 reduce-scatter.1
where the time goes:
time: 214 us; the launch traced here: 212 us
  waiting for transfers between devices  117 us (55%)
  starting transfers between devices  39.2 us (18%)
  matrix products  25.8 us (12%)
  between operations  15.6 us (7%)
  local copies, waits for them, and re-layouts  8.5 us (4%)
  other arithmetic  6.22 us (3%)
    reduce_scatter x1, waiting for transfers between devices, shards(): lax.psum_scatter(lax.dot_general(columns, grad_qkv_tok, contract_first, p...  43.4 us
    all_gather x1, waiting for transfers between devices, sent_together(): lax.all_gather(both, axis, axis=dim, tiled=True)  33.6 us
    all_to_all x2, waiting for transfers between devices, from_everyone(): lax.all_to_all(jnp.broadcast_to(array[None], (peers, *array.shape)), axis...  20.6 us
    ppermute x6, starting transfers between devices, shifted(): return lax.ppermute(value, axis, pairs)  19.5 us
    ppermute x6, waiting for transfers between devices, shifted(): return lax.ppermute(value, axis, pairs)  18.5 us
    all_to_all x2, starting transfers between devices, from_everyone(): lax.all_to_all(jnp.broadcast_to(array[None], (peers, *array.shape)), axis...  14.5 us
    all_to_all x1, starting transfers between devices, sum_at_owner(): lax.all_to_all(blocks, axis, split_axis=0, concat_axis=0, tiled=True)  5.15 us
  transfers between devices with their start and end apart: 11, of which 10 were waited for; matrix products, arithmetic and copies ran while one was open for 8% of the time, Pallas kernels for 0%

commit v1 on v0

v1 whole, which is shorter than its diff:
```python
import functools

import jax
import jax.numpy as jnp
from jax import lax
from jax.experimental import pallas as pl
from jax.experimental.pallas import tpu as pltpu
from jax.sharding import PartitionSpec as P

EPSILON = 1e-05
SCALE = 32 ** (-0.5)
MESH = pl.DeviceIdType.MESH
F32 = jnp.float32
BF16 = jnp.bfloat16
D = 768
HALF = 384
COLS = 4 * HALF
CHUNK = 48
TOK = 128

BACK = (0, 8, 1, 9)


def dot(a, b):
    return jnp.dot(a, b, preferred_element_type=F32)


def dot_t(a, b):
    return lax.dot_general(a, b, (((1,), (1,)), ((), ())), preferred_element_type=F32)


def t_dot(a, b):
    return lax.dot_general(a, b, (((0,), (0,)), ((), ())), preferred_element_type=F32)


def block_source(block_row, flag):
    group = (block_row >> 4) & 3
    n = block_row & 15
    east = group >> 1
    high = 1 - ((group & 1) ^ (flag * east))
    row = (n >> 2) + 4 * high
    col = (n & 3) + 4 * (1 - east)
    return ((block_row >> 6) << 6) + row * 8 + col


def body(
    tok_ref, upi_ref, wq_ref, wp_ref, codes_ref,
    out_ref, gt_ref, gqo_ref, gpo_ref,
    blocks, win, stage, wsib, wbuf, hid, ups, norm, inv_ref, qkv, back, mixed, gtok, opart,
    xs, xr, rsend, rrecv, grad, h2, f2, h1, f1, zs, zr, zo, za,
    roll_s, roll_r, w_s, w_r, ga_s, ga_r, gb_s, gb_r, sib_s, sib_r, par_s, par_r, ret_s, ret_r,
    h2_s, h2_r, f2_s, f2_r, h1_s, h1_r, f1_s, f1_r, z1_s, z1_r, z2_s, z2_r,
):
    rep = lax.axis_index("rep")
    lev = lax.axis_index("lev")
    tile = lax.axis_index("tile")
    core = tile % 2
    chip = tile // 2
    x = chip % 4
    y = chip // 4
    z = lev * 2 + rep
    sib_tile = chip * 2 + (1 - core)
    sib = (rep, lev, sib_tile)
    p = jnp.where(core == 0, x, y)
    q = jnp.where(core == 0, y, x)
    sp = 1 + 3 * core
    sq = 4 - 3 * core

    def chip_at(dp, dq):
        return ((p + dp + 4) % 4) * sp + ((q + dq + 4) % 4) * sq

    def at(dp, dq):
        return (rep, lev, chip_at(dp, dq) * 2 + core)

    def at_z(d, which):
        other = (z + d) % 8
        return (other % 2, other // 2, chip * 2 + which)

    def rolled(dl, dt):
        return (rep, (lev + dl + 4) % 4, (tile + dt + 32) % 32)

    def copy(src, dst, ssem, rsem, where):
        return pltpu.make_async_remote_copy(
            src_ref=src, dst_ref=dst, send_sem=ssem, recv_sem=rsem, device_id=where, device_id_type=MESH
        )

    started = []

    def send(src, dst, ssem, rsem, where):
        c = copy(src, dst, ssem, rsem, where)
        c.start()
        started.append(c)

    def arrived(dst, ssem, rsem):
        copy(dst, dst, ssem, rsem, sib).wait_recv()

    barrier = pltpu.get_barrier_semaphore()
    partners = [sib]
    partners += [(rep, lev, (y * 4 + (x + d) % 4) * 2 + core) for d in (1, 3)]
    partners += [rolled(0, dt) for dt in (1, -1, 8, -8, 9, -9)]
    partners += [rolled(-1, -dt) for dt in (1, 8, 9)] + [rolled(1, dt) for dt in (1, 8, 9)]
    partners += [at_z(d, core) for d in range(1, 8)]
    partners += [at_z(d, 1 - core) for d in range(1, 8)]
    for partner in partners:
        pl.semaphore_signal(barrier, inc=1, device_id=partner, device_id_type=MESH)

    for half in range(2):
        for kind in range(3):
            stage[half, :, kind * HALF:(kind + 1) * HALF] = wq_ref[:, kind * D + half * HALF:kind * D + (half + 1) * HALF]
        stage[half, :, 3 * HALF:] = wp_ref[:, half * HALF:(half + 1) * HALF]
    flag = codes_ref[(tile + 31) % 32, 0]
    rows_i = lax.broadcasted_iota(jnp.int32, (TOK, TOK), 0)
    cols_i = lax.broadcasted_iota(jnp.int32, (TOK, TOK), 1)
    order = (cols_i == block_source(rows_i, flag)).astype(F32).astype(BF16)
    blocks[:, :D] = dot(order, tok_ref[...]).astype(BF16)
    blocks[:, D:] = dot(order, upi_ref[...]).astype(BF16)
    pl.semaphore_wait(barrier, len(partners))

    send(stage.at[1 - core], wsib, w_s, w_r, sib)

    def span(level, group):
        return pl.ds(level * 64 + group * 16, 16)

    for level in (0, 1):
        for group in range(4):
            if level == 1 and group == 0:
                continue
            n = (1 - level) * 4 + group
            send(blocks.at[span(level, group)], win.at[span(1 - level, group)], roll_s.at[n], roll_r.at[n],
                 rolled(level - 1, -BACK[group]))
    win[0:16, :] = blocks[64:80, :]

    arrived(wsib, w_s, w_r)
    mine = stage[core].astype(F32)
    other = wsib[...].astype(F32)
    first = jnp.where(core == 0, mine, other)
    second = jnp.where(core == 0, other, mine)

    def rows_of(dp, dq):
        return pl.ds(pl.multiple_of(chip_at(dp, dq) * CHUNK, 16), CHUNK)

    wbuf[rows_of(0, 0), :] = jnp.concatenate([first, second], axis=0).astype(BF16)

    def w_at(dp, dq, half=None):
        if half is None:
            return wbuf.at[rows_of(dp, dq)]
        return wbuf.at[rows_of(dp, dq), pl.ds(half * D, D)]

    def fan_out(k, dp):
        send(w_at(dp, 0), w_at(dp, 0), gb_s.at[k, 0], gb_r.at[k, 0], at(0, 1))
        send(w_at(dp, 0), w_at(dp, 0), gb_s.at[k, 1], gb_r.at[k, 1], at(0, -1))

    def relay(k, dp):
        arrived(w_at(dp, -1), gb_s.at[k, 0], gb_r.at[k, 0])
        send(w_at(dp, -1, 0), w_at(dp, -1, 0), gb_s.at[k, 2], gb_r.at[k, 2], at(0, 1))
        arrived(w_at(dp, 1), gb_s.at[k, 1], gb_r.at[k, 1])
        send(w_at(dp, 1, 1), w_at(dp, 1, 1), gb_s.at[k, 3], gb_r.at[k, 3], at(0, -1))

    send(w_at(0, 0), w_at(0, 0), ga_s.at[0], ga_r.at[0], at(1, 0))
    send(w_at(0, 0), w_at(0, 0), ga_s.at[1], ga_r.at[1], at(-1, 0))
    fan_out(0, 0)
    arrived(w_at(-1, 0), ga_s.at[0], ga_r.at[0])
    send(w_at(-1, 0, 0), w_at(-1, 0, 0), ga_s.at[2], ga_r.at[2], at(1, 0))
    fan_out(1, -1)
    arrived(w_at(1, 0), ga_s.at[1], ga_r.at[1])
    send(w_at(1, 0, 1), w_at(1, 0, 1), ga_s.at[3], ga_r.at[3], at(-1, 0))
    fan_out(2, 1)
    relay(0, 0)
    arrived(w_at(2, 0, 0), ga_s.at[2], ga_r.at[2])
    arrived(w_at(2, 0, 1), ga_s.at[3], ga_r.at[3])
    fan_out(3, 2)
    relay(1, -1)
    relay(2, 1)

    for n in range(1, 8):
        arrived(win.at[pl.ds(n * 16, 16)], roll_s.at[n], roll_r.at[n])
    my_rows = pl.ds(pl.multiple_of(core * TOK, TOK), TOK)
    ups[my_rows, :] = win[:, D:]
    send(ups.at[my_rows], ups.at[my_rows], sib_s.at[1], sib_r.at[1], sib)
    values = win[:, :D].astype(F32)
    centred = values - jnp.mean(values, axis=1, keepdims=True)
    inverse = lax.rsqrt(jnp.mean(jnp.square(centred), axis=1, keepdims=True) + EPSILON)
    normalized = centred * inverse
    norm[...] = normalized
    inv_ref[...] = jnp.broadcast_to(inverse, (TOK, 128))
    hid[my_rows, :] = normalized.astype(BF16)
    send(hid.at[my_rows], hid.at[my_rows], sib_s.at[0], sib_r.at[0], sib)
    relay(3, 2)
    their_rows = pl.ds(pl.multiple_of((1 - core) * TOK, TOK), TOK)
    arrived(hid.at[their_rows], sib_s.at[0], sib_r.at[0])
    arrived(ups.at[their_rows], sib_s.at[1], sib_r.at[1])
    for k, dp in enumerate((0, -1, 1, 2)):
        arrived(w_at(dp, 2, 0), gb_s.at[k, 2], gb_r.at[k, 2])
        arrived(w_at(dp, 2, 1), gb_s.at[k, 3], gb_r.at[k, 3])

    qkv[...] = dot(hid[...], wbuf[:, :3 * HALF]).astype(BF16)
    back[...] = dot(ups[...], wbuf[:, 3 * HALF:]).astype(BF16)
    allow = jnp.where(lev == 3, jnp.where((rows_i >> 6) == (cols_i >> 6), 1.0, 0.0), 1.0).astype(F32)
    allow = jnp.concatenate([allow] * 4, axis=0)
    lane_head = lax.broadcasted_iota(jnp.int32, (TOK, 128), 1) >> 5
    head_masks = [(lane_head == h).astype(F32).astype(BF16) for h in range(4)]

    def stacked(part):
        return jnp.concatenate([part * m for m in head_masks], axis=0)

    def beside(part):
        return jnp.concatenate([part[h * TOK:(h + 1) * TOK] for h in range(4)], axis=1)

    for w in range(2):
        rows = slice(w * TOK, (w + 1) * TOK)
        for j in range(3):
            lanes = [slice(kind * HALF + j * 128, kind * HALF + (j + 1) * 128) for kind in range(3)]
            query, key, value = (qkv[rows, s] for s in lanes)
            coming = back[rows, lanes[0]]
            query_s, key_s, value_s, coming_s = (stacked(a) for a in (query, key, value, coming))
            raised = jnp.exp(dot_t(query_s, key) * SCALE) * allow
            prob = raised * (1.0 / jnp.sum(raised, axis=1, keepdims=True))
            low = prob.astype(BF16)
            mixed[rows, lanes[0]] = dot(beside(low), value_s).astype(BF16)
            grad_prob = dot_t(coming_s, value)
            centre = jnp.sum(prob * grad_prob, axis=1, keepdims=True)
            grad_scores = (prob * (grad_prob - centre) * SCALE).astype(BF16)
            gtok[rows, lanes[0]] = dot(beside(grad_scores), key_s).astype(BF16)
            gtok[rows, lanes[1]] = t_dot(grad_scores, query_s).astype(BF16)
            gtok[rows, lanes[2]] = t_dot(low, coming_s).astype(BF16)

    grad[:, :3 * HALF] = t_dot(hid[...], gtok[...]).astype(BF16)
    grad[:, 3 * HALF:] = t_dot(ups[...], mixed[...]).astype(BF16)

    def g_at(dp, dq, half=None):
        if half is None:
            return grad.at[rows_of(dp, dq)]
        return grad.at[rows_of(dp, dq), pl.ds(half * D, D)]

    along = (2, 1, -1, 0)
    for k, dp in enumerate(along):
        send(g_at(dp, 2, 0), h2.at[0, k], h2_s.at[0, k], h2_r.at[0, k], at(0, 1))
        send(g_at(dp, 2, 1), h2.at[1, k], h2_s.at[1, k], h2_r.at[1, k], at(0, -1))

    opart[:, :D] = dot_t(mixed[...], wbuf[:, 3 * HALF:])
    opart[:, D:] = dot_t(gtok[...], wbuf[:, :3 * HALF])
    xs[...] = opart[their_rows, :].astype(BF16)
    send(xs, xr, par_s, par_r, sib)

    def add_half(dp, dq, half, k):
        where = (rows_of(dp, dq), pl.ds(half * D, D))
        grad[where] = (grad[where].astype(F32) + h2[half, k].astype(F32)).astype(BF16)

    for k, dp in enumerate(along):
        arrived(h2.at[0, k], h2_s.at[0, k], h2_r.at[0, k])
        add_half(dp, 1, 0, k)
        send(g_at(dp, 1), f2.at[0, k], f2_s.at[0, k], f2_r.at[0, k], at(0, 1))
        arrived(h2.at[1, k], h2_s.at[1, k], h2_r.at[1, k])
        add_half(dp, -1, 1, k)
        send(g_at(dp, -1), f2.at[1, k], f2_s.at[1, k], f2_r.at[1, k], at(0, -1))

    arrived(xr, par_s, par_r)
    total = win[:, :D].astype(F32) + opart[my_rows, :D] + xr[:, :D].astype(F32)
    rsend[:, :D] = total.astype(BF16)
    grad_hidden = opart[my_rows, D:] + xr[:, D:].astype(F32)
    normalized = norm[...]
    centre = jnp.mean(grad_hidden, axis=1, keepdims=True)
    along_norm = jnp.mean(grad_hidden * normalized, axis=1, keepdims=True)
    moved = (grad_hidden - centre - normalized * along_norm) * inv_ref[:, :1]
    rsend[:, D:] = (win[:, D:].astype(F32) + moved).astype(BF16)
    for level in (0, 1):
        for group in range(4):
            if level == 1 and group == 0:
                continue
            n = level * 4 + group if level == 0 else 4 + group
            send(rsend.at[span(1 - level, group)], rrecv.at[span(level, group)], ret_s.at[n], ret_r.at[n],
                 rolled(1 - level, BACK[group]))
    rrecv[64:80, :] = rsend[0:16, :]

    def sum_second(k, dp):
        arrived(f2.at[0, k], f2_s.at[0, k], f2_r.at[0, k])
        arrived(f2.at[1, k], f2_s.at[1, k], f2_r.at[1, k])
        return grad[rows_of(dp, 0), :].astype(F32) + f2[0, k].astype(F32) + f2[1, k].astype(F32)

    grad[rows_of(2, 0), :] = sum_second(0, 2).astype(BF16)
    send(g_at(2, 0, 0), h1.at[0], h1_s.at[0], h1_r.at[0], at(1, 0))
    send(g_at(2, 0, 1), h1.at[1], h1_s.at[1], h1_r.at[1], at(-1, 0))
    for side, dp in ((0, 1), (1, -1)):
        partial = sum_second(1 + side, dp)
        arrived(h1.at[side], h1_s.at[side], h1_r.at[side])
        grad[rows_of(dp, 0), :] = partial.astype(BF16)
        where = (rows_of(dp, 0), pl.ds(side * D, D))
        grad[where] = (partial[:, side * D:(side + 1) * D] + h1[side].astype(F32)).astype(BF16)
        send(g_at(dp, 0), f1.at[side], f1_s.at[side], f1_r.at[side], at(dp, 0))
    plane = sum_second(3, 0)
    for side in range(2):
        arrived(f1.at[side], f1_s.at[side], f1_r.at[side])
        plane = plane + f1[side].astype(F32)

    for piece in range(8):
        kind, r = piece // 2, piece % 2
        zs[piece] = plane[r * 24:(r + 1) * 24, kind * HALF:(kind + 1) * HALF].astype(BF16)
    for d in range(1, 8):
        send(zs.at[(z + d) % 8], zr.at[d], z1_s.at[d], z1_r.at[d], at_z(d, core))

    for n in range(8):
        if n != 4:
            arrived(rrecv.at[pl.ds(n * 16, 16)], ret_s.at[n], ret_r.at[n])
    order_t = (rows_i == block_source(cols_i, flag)).astype(F32).astype(BF16)
    out_ref[...] = dot(order_t, rrecv[:, :D]).astype(BF16)
    gt_ref[...] = dot(order_t, rrecv[:, D:]).astype(BF16)

    total = zs[z].astype(F32)
    for d in range(1, 8):
        arrived(zr.at[d], z1_s.at[d], z1_r.at[d])
        total = total + zr[d].astype(F32)
    zo[...] = total.astype(BF16)
    r = z % 2
    slot = (z // 2) * 2 + core
    last = [copy(zo, za.at[slot], z2_s.at[d], z2_r.at[slot], at_z(d, r)) for d in range(8)]
    for d in range(1, 8):
        last[d].start()

    @pl.when(r == core)
    def _():
        za[slot] = zo[...]

    @pl.when(r != core)
    def _():
        last[0].start()

    for n in range(8):
        own = jnp.logical_and(r == core, slot == n)

        @pl.when(jnp.logical_not(own))
        def _():
            arrived(za.at[n], z2_s.at[0], z2_r.at[n])

    for kind in range(4):
        for half in range(2):
            piece = za[kind * 2 + half].astype(F32)
            if kind < 3:
                gqo_ref[:, kind * D + half * HALF:kind * D + (half + 1) * HALF] = piece
            else:
                gpo_ref[:, half * HALF:(half + 1) * HALF] = piece

    for c in started + last[1:]:
        c.wait_send()

    @pl.when(r != core)
    def _():
        last[0].wait_send()


def shards(tokens, w_qkv, w_proj, seam_codes, upstream):
    dma = pltpu.SemaphoreType.DMA
    vmem = pltpu.VMEM
    scratch = [
        vmem((TOK, 2 * D), BF16),
        vmem((TOK, 2 * D), BF16),
        vmem((2, 24, COLS), BF16),
        vmem((24, COLS), BF16),
        vmem((D, COLS), BF16),
        vmem((2 * TOK, D), BF16),
        vmem((2 * TOK, D), BF16),
        vmem((TOK, D), F32),
        vmem((TOK, 128), F32),
        vmem((2 * TOK, 3 * HALF), BF16),
        vmem((2 * TOK, HALF), BF16),
        vmem((2 * TOK, HALF), BF16),
        vmem((2 * TOK, 3 * HALF), BF16),
        vmem((2 * TOK, 2 * D), F32),
        vmem((TOK, 2 * D), BF16),
        vmem((TOK, 2 * D), BF16),
        vmem((TOK, 2 * D), BF16),
        vmem((TOK, 2 * D), BF16),
        vmem((D, COLS), BF16),
        vmem((2, 4, CHUNK, D), BF16),
        vmem((2, 4, CHUNK, COLS), BF16),
        vmem((2, CHUNK, D), BF16),
        vmem((2, CHUNK, COLS), BF16),
        vmem((8, 24, HALF), BF16),
        vmem((8, 24, HALF), BF16),
        vmem((24, HALF), BF16),
        vmem((8, 24, HALF), BF16),
        dma((8,)), dma((8,)),
        dma, dma,
        dma((4,)), dma((4,)),
        dma((4, 4)), dma((4, 4)),
        dma((2,)), dma((2,)),
        dma, dma,
        dma((8,)), dma((8,)),
        dma((2, 4)), dma((2, 4)), dma((2, 4)), dma((2, 4)),
        dma((2,)), dma((2,)), dma((2,)), dma((2,)),
        dma((8,)), dma((8,)), dma((8,)), dma((8,)),
    ]
    in_vmem = pl.BlockSpec(memory_space=pltpu.VMEM)
    out, grad_tok, grad_qkv, grad_proj = pl.pallas_call(
        body,
        out_shape=(
            jax.ShapeDtypeStruct((TOK, D), BF16),
            jax.ShapeDtypeStruct((TOK, D), BF16),
            jax.ShapeDtypeStruct((24, 3 * D), F32),
            jax.ShapeDtypeStruct((24, D), F32),
        ),
        in_specs=[in_vmem] * 4 + [pl.BlockSpec(memory_space=pltpu.SMEM)],
        out_specs=(in_vmem,) * 4,
        scratch_shapes=scratch,
        compiler_params=pltpu.CompilerParams(
            collective_id=0, has_side_effects=True, vmem_limit_bytes=48 * 1024 * 1024
        ),
        name="layer",
    )(tokens.reshape(TOK, D), upstream.reshape(TOK, D), w_qkv, w_proj, seam_codes)
    return (out.reshape(tokens.shape), grad_tok.reshape(tokens.shape), grad_qkv, grad_proj)


def solution(mesh):
    field = P("rep", "lev", "tile", None, None, None)
    rows = P("tile", None)
    return jax.shard_map(
        shards,
        mesh=mesh,
        in_specs=(field, rows, rows, P(), field),
        out_specs=(field, field, rows, rows),
        check_vma=False,
    )
```

time: 214 us -> 77 us (0.36)
  waiting for transfers between devices: 117 us -> 0 us
  Pallas kernels: 0 us -> 68.6 us
  starting transfers between devices: 39.2 us -> 0 us
  matrix products: 25.8 us -> 0 us
  between operations: 15.6 us -> 0.65 us
  other arithmetic: 6.22 us -> 0 us
    pallas_call x0 -> x1, Pallas kernels: none -> 68.6 us  [shards(): pl.pallas_call(body, out_shape=(jax.ShapeDtypeStruct((TOK, D), BF16), jax...]
    reduce_scatter x1 -> x0, waiting for transfers between devices: 43.4 us -> none  [shards(): lax.psum_scatter(lax.dot_general(columns, grad_qkv_tok, contract_first, p...]
    all_gather x1 -> x0, waiting for transfers between devices: 33.6 us -> none  [sent_together(): lax.all_gather(both, axis, axis=dim, tiled=True)]
    dot_general x12 -> x0, matrix products: 24 us -> none  [the longest x1 3.4 us: shards(): lax.dot_general(grad_qkv_tok, full_qkv, contract_last, preferred_element_...]
    all_to_all x3 -> x0, waiting for transfers between devices: 21.1 us -> none  [the longest x2 20.6 us: from_everyone(): lax.all_to_all(jnp.broadcast_to(array[None], (peers, *array.shape)), axis...]
    all_to_all x3 -> x0, starting transfers between devices: 19.6 us -> none  [the longest x2 14.5 us: from_everyone(): lax.all_to_all(jnp.broadcast_to(array[None], (peers, *array.shape)), axis...]
    ppermute x6 -> x0, starting transfers between devices: 19.5 us -> none  [shifted(): return lax.ppermute(value, axis, pairs)]
    ppermute x6 -> x0, waiting for transfers between devices: 18.5 us -> none  [shifted(): return lax.ppermute(value, axis, pairs)]
  transfers between devices with their start and end apart: 11 -> 0, of which waited for: 10 -> 0; matrix products, arithmetic and copies ran while one was open for 8% -> 0% of each run, Pallas kernels for 0% -> 0%
where the time goes in v1:
time: 77 us; the launch traced here: 76.2 us
  Pallas kernels  68.6 us (89%)
  local copies, waits for them, and re-layouts  6.95 us (9%)
    pallas_call x1, Pallas kernels, shards(): pl.pallas_call(body, out_shape=(jax.ShapeDtypeStruct((TOK, D), BF16), jax...  68.6 us
    unnamed x15, local copies, waits for them, and re-layouts  6.95 us

profile of v1, /device:TPU:1, one launch (start us, length us, event | category | flops | bytes accessed | tf_op | source)
XLA Modules:
  0.0 76.2 jit_solution(4931560083518740820)
XLA Ops:
  0.6 0.0 copy-start.4
  0.6 0.7 copy-done.4
  1.3 0.1 copy.9.codes_ref
  1.4 0.0 copy-start
  1.4 0.9 %copy-done = bf16[1,2,1,8,8,768]{5,4,3,2,1,0:T(8,128)(2,1)S(1)} copy-done((bf16[1,2,1,8,8,768]{5,4,3,2,1,0:T(8,128)(2,1)S(1)}, bf16[1,2,1,8,8,768]{5,4,3,2,1,0:T(8,128)(2,1)}, u32[]{:S(2)}) %copy-start) | copy-done | bytes 196632
  2.3 0.0 copy-start.1
  2.3 0.9 %copy-done.1 = bf16[1,2,1,8,8,768]{5,4,3,2,1,0:T(8,128)(2,1)S(1)} copy-done((bf16[1,2,1,8,8,768]{5,4,3,2,1,0:T(8,128)(2,1)S(1)}, bf16[1,2,1,8,8,768]{5,4,3,2,1,0:T(8,128)(2,1)}, u32[]{:S(2)}) %copy-start.1) | copy-done | bytes 196632
  3.3 0.0 copy-start.2
  3.3 0.9 %copy-done.2 = bf16[24,2304]{1,0:T(8,128)(2,1)S(1)} copy-done((bf16[24,2304]{1,0:T(8,128)(2,1)S(1)}, bf16[24,2304]{1,0:T(8,128)(2,1)}, u32[]{:S(2)}) %copy-start.2) | copy-done | bytes 110616
  4.2 0.0 copy-start.3
  4.2 0.8 %copy-done.3 = bf16[24,768]{1,0:T(8,128)(2,1)S(1)} copy-done((bf16[24,768]{1,0:T(8,128)(2,1)S(1)}, bf16[24,768]{1,0:T(8,128)(2,1)}, u32[]{:S(2)}) %copy-start.3) | copy-done | bytes 36888
  4.9 68.6 %layer.1 = (bf16[128,768]{1,0:T(8,128)(2,1)S(1)}, bf16[128,768]{1,0:T(8,128)(2,1)S(1)}, f32[24,2304]{1,0:T(8,128)S(1)}, f32[24,768]{1,0:T(8,128)S(1)}) custom-call(bf16[128,768]{1,0:T(8,128)(2,1)S(1)} %bitcast.8, bf16[128,768]{1,0:T(8,128)(2,1)S(1)} %bitcast.9, bf16[24,2304]{1,0:T(8,128)(2,1)S(1)} %copy-done.2, bf16[24,768]{1,0:T(8,128)(2,1)S(1)} %copy-done.3, ...), custom_call_target="tpu_custom_call" | custom-call | tf_op jit(solution)/shard_map/layer/pallas_call | solution.py:393
  73.5 0.7 copy.16
  74.2 0.7 copy.17
  74.8 0.7 copy.18
  75.5 0.6 copy.19
Async XLA Ops:
  0.6 0.7 copy-start.4
  1.4 0.9 %copy-start = (bf16[1,2,1,8,8,768]{5,4,3,2,1,0:T(8,128)(2,1)S(1)}, bf16[1,2,1,8,8,768]{5,4,3,2,1,0:T(8,128)(2,1)}, u32[]{:S(2)}) copy-start(bf16[1,2,1,8,8,768]{5,4,3,2,1,0:T(8,128)(2,1)} %param.5) | copy-start | bytes 589828
  2.3 0.9 %copy-start.1 = (bf16[1,2,1,8,8,768]{5,4,3,2,1,0:T(8,128)(2,1)S(1)}, bf16[1,2,1,8,8,768]{5,4,3,2,1,0:T(8,128)(2,1)}, u32[]{:S(2)}) copy-start(bf16[1,2,1,8,8,768]{5,4,3,2,1,0:T(8,128)(2,1)} %param.9) | copy-start | bytes 589828
  3.3 0.9 %copy-start.2 = (bf16[24,2304]{1,0:T(8,128)(2,1)S(1)}, bf16[24,2304]{1,0:T(8,128)(2,1)}, u32[]{:S(2)}) copy-start(bf16[24,2304]{1,0:T(8,128)(2,1)} %wq_ref.1) | copy-start | bytes 331780
  4.2 0.8 %copy-start.3 = (bf16[24,768]{1,0:T(8,128)(2,1)S(1)}, bf16[24,768]{1,0:T(8,128)(2,1)}, u32[]{:S(2)}) copy-start(bf16[24,768]{1,0:T(8,128)(2,1)} %wp_ref.1) | copy-start | bytes 110596

commit v2 on v1

v2 whole, which is shorter than its diff:
```python
import functools

import jax
import jax.numpy as jnp
from jax import lax
from jax.experimental import pallas as pl
from jax.experimental.pallas import tpu as pltpu
from jax.sharding import PartitionSpec as P

EPSILON = 1e-05
SCALE = 32 ** (-0.5)
MESH = pl.DeviceIdType.MESH
F32 = jnp.float32
BF16 = jnp.bfloat16
D = 768
HALF = 384
COLS = 4 * HALF
GROUPS = 3
WIDE = COLS // GROUPS
CHUNK = 48
TOK = 128

BACK = (0, 8, 1, 9)


def dot(a, b):
    return jnp.dot(a, b, preferred_element_type=F32)


def dot_t(a, b):
    return lax.dot_general(a, b, (((1,), (1,)), ((), ())), preferred_element_type=F32)


def t_dot(a, b):
    return lax.dot_general(a, b, (((0,), (0,)), ((), ())), preferred_element_type=F32)


def block_source(block_row, flag):
    group = (block_row >> 4) & 3
    n = block_row & 15
    east = group >> 1
    high = 1 - ((group & 1) ^ (flag * east))
    row = (n >> 2) + 4 * high
    col = (n & 3) + 4 * (1 - east)
    return ((block_row >> 6) << 6) + row * 8 + col


def body(
    tok_hbm, upi_hbm, wq_hbm, wp_hbm, codes_hbm,
    out_hbm, gt_hbm, gqo_hbm, gpo_hbm,
    tok, upi, wq, wp, codes, blocks, win, stage, wsib, wbuf, wnat, hid, ups, hid_t, ups_t, norm, inv_ref,
    qkv, back, mixed, gtok, opart, xs, xr, rsend, rrecv, grad, h2, f2, psum, f1, zs, zr, zo, za,
    out_v, gt_v, gqo_v, gpo_v,
    in_sem, out_sem,
    roll_s, roll_r, w_s, w_r, ga_s, ga_r, gb_s, gb_r, sib_s, sib_r, par_s, par_r, ret_s, ret_r,
    h2_s, h2_r, f2_s, f2_r, f1_s, f1_r, z1_s, z1_r, z2_s, z2_r,
):
    fetched = [
        pltpu.make_async_copy(a, b, in_sem.at[i])
        for i, (a, b) in enumerate(((wq_hbm, wq), (wp_hbm, wp), (codes_hbm, codes), (tok_hbm, tok), (upi_hbm, upi)))
    ]
    for c in fetched:
        c.start()

    rep = lax.axis_index("rep")
    lev = lax.axis_index("lev")
    tile = lax.axis_index("tile")
    core = tile % 2
    chip = tile // 2
    x = chip % 4
    y = chip // 4
    z = lev * 2 + rep
    sib = (rep, lev, chip * 2 + (1 - core))
    p = jnp.where(core == 0, x, y)
    q = jnp.where(core == 0, y, x)
    sp = 1 + 3 * core
    sq = 4 - 3 * core

    def around(value, step):
        return (value + step + 4) % 4

    def at(dp, dq):
        return (rep, lev, (around(p, dp) * sp + around(q, dq) * sq) * 2 + core)

    def at_z(d, where):
        other = (z + d + 8) % 8
        return (other % 2, other // 2, where)

    def near(dz, dt):
        return at_z(dz, (tile + dt + 32) % 32)

    def copy(src, dst, ssem, rsem, where):
        return pltpu.make_async_remote_copy(
            src_ref=src, dst_ref=dst, send_sem=ssem, recv_sem=rsem, device_id=where, device_id_type=MESH
        )

    started = []

    def send(src, dst, ssem, rsem, where):
        c = copy(src, dst, ssem, rsem, where)
        c.start()
        started.append(c)

    def arrived(dst, ssem, rsem):
        copy(dst, dst, ssem, rsem, sib).wait_recv()

    barrier = pltpu.get_barrier_semaphore()
    partners = [sib]
    partners += [at(d, 0) for d in (1, 2, 3)] + [at(0, d) for d in (1, 2, 3)]
    partners += [near(dz, dt) for dz in (1, -1) for dt in (1, -1, 8, -8, 9, -9)]
    partners += [at_z(d, chip * 2 + c) for d in range(1, 8) for c in (0, 1)]
    for partner in partners:
        pl.semaphore_signal(barrier, inc=1, device_id=partner, device_id_type=MESH)

    fetched[0].wait()
    fetched[1].wait()
    for half in range(2):
        for j in range(GROUPS):
            for kind in range(3):
                at_col = kind * D + half * HALF + j * 128
                stage[half, :, j * WIDE + kind * 128:j * WIDE + (kind + 1) * 128] = wq[:, at_col:at_col + 128]
            at_col = half * HALF + j * 128
            stage[half, :, j * WIDE + 384:(j + 1) * WIDE] = wp[:, at_col:at_col + 128]
    for c in fetched[2:]:
        c.wait()
    flag = codes[0, (tile + 31) % 32]
    rows_i = lax.broadcasted_iota(jnp.int32, (TOK, TOK), 0)
    cols_i = lax.broadcasted_iota(jnp.int32, (TOK, TOK), 1)
    order = (cols_i == block_source(rows_i, flag)).astype(F32).astype(BF16)
    blocks[:, :D] = dot(order, tok[...]).astype(BF16)
    blocks[:, D:] = dot(order, upi[...]).astype(BF16)
    pl.semaphore_wait(barrier, len(partners))

    send(stage.at[1 - core], wsib, w_s, w_r, sib)

    def span(level, group):
        return pl.ds(level * 64 + group * 16, 16)

    for group in range(4):
        for level, dz in ((1, 1), (0, -1)):
            n = (1 - level) * 4 + group
            send(blocks.at[span(level, group)], win.at[span(1 - level, group)], roll_s.at[n], roll_r.at[n],
                 near(dz, -BACK[group]))

    arrived(wsib, w_s, w_r)
    mine = stage[core].astype(F32)
    other = wsib[...].astype(F32)
    first = jnp.where(core == 0, mine, other)
    second = jnp.where(core == 0, other, mine)
    chunk = jnp.concatenate([first, second], axis=0).astype(BF16)
    for j in range(GROUPS):
        wbuf[j, q * 4 + p] = chunk[:, j * WIDE:(j + 1) * WIDE]

    def line(buf, j, dq, start=0, count=4):
        return buf.at[j, pl.ds(around(q, dq) * 4 + start, count)]

    def gather_first(j):
        own = wbuf.at[j, q * 4 + p]
        for d in (1, 3, 2):
            send(own, own, ga_s.at[j, d], ga_r.at[j, d], at(d, 0))

    def gather_second(j):
        for d in (1, 2, 3):
            arrived(wbuf.at[j, q * 4 + around(p, -d)], ga_s.at[j, d], ga_r.at[j, d])
        send(line(wbuf, j, 0), line(wbuf, j, 0), gb_s.at[j, 0], gb_r.at[j, 0], at(0, 1))
        send(line(wbuf, j, 0), line(wbuf, j, 0), gb_s.at[j, 1], gb_r.at[j, 1], at(0, -1))

    def gather_relay(j):
        arrived(line(wbuf, j, -1), gb_s.at[j, 0], gb_r.at[j, 0])
        send(line(wbuf, j, -1, 0, 2), line(wbuf, j, -1, 0, 2), gb_s.at[j, 2], gb_r.at[j, 2], at(0, 1))
        arrived(line(wbuf, j, 1), gb_s.at[j, 1], gb_r.at[j, 1])
        send(line(wbuf, j, 1, 2, 2), line(wbuf, j, 1, 2, 2), gb_s.at[j, 3], gb_r.at[j, 3], at(0, -1))

    def natural(n):
        return n + core * ((n % 4) * 4 + n // 4 - n)

    def gather_end(j):
        arrived(line(wbuf, j, 2, 0, 2), gb_s.at[j, 2], gb_r.at[j, 2])
        arrived(line(wbuf, j, 2, 2, 2), gb_s.at[j, 3], gb_r.at[j, 3])
        for n in range(16):
            wnat[j, n * CHUNK:(n + 1) * CHUNK, :] = wbuf[j, natural(n)]

    for j in range(GROUPS):
        gather_first(j)
    for j in range(GROUPS):
        gather_second(j)
    gather_relay(0)

    for n in range(8):
        arrived(win.at[pl.ds(n * 16, 16)], roll_s.at[n], roll_r.at[n])
    my_rows = pl.ds(pl.multiple_of(core * TOK, TOK), TOK)
    their_rows = pl.ds(pl.multiple_of((1 - core) * TOK, TOK), TOK)
    ups[my_rows, :] = win[:, D:]
    send(ups.at[my_rows], ups.at[my_rows], sib_s.at[1], sib_r.at[1], sib)
    values = win[:, :D].astype(F32)
    centred = values - jnp.mean(values, axis=1, keepdims=True)
    inverse = lax.rsqrt(jnp.mean(jnp.square(centred), axis=1, keepdims=True) + EPSILON)
    normalized = centred * inverse
    norm[...] = normalized
    inv_ref[...] = jnp.broadcast_to(inverse, (TOK, 128))
    hid[my_rows, :] = normalized.astype(BF16)
    send(hid.at[my_rows], hid.at[my_rows], sib_s.at[0], sib_r.at[0], sib)
    gather_relay(1)
    arrived(ups.at[their_rows], sib_s.at[1], sib_r.at[1])
    arrived(hid.at[their_rows], sib_s.at[0], sib_r.at[0])
    hid_t[...] = hid[...].T
    ups_t[...] = ups[...].T

    wrapped = jnp.logical_or(z == 0, z == 7)
    allow = jnp.where(wrapped, jnp.where((rows_i >> 6) == (cols_i >> 6), 1.0, 0.0), 1.0).astype(F32)
    allow = jnp.concatenate([allow] * 4, axis=0)
    lane_head = lax.broadcasted_iota(jnp.int32, (TOK, 128), 1) >> 5
    head_masks = [(lane_head == h).astype(F32).astype(BF16) for h in range(4)]

    def stacked(part):
        return jnp.concatenate([part * m for m in head_masks], axis=0)

    def beside(part):
        return jnp.concatenate([part[h * TOK:(h + 1) * TOK] for h in range(4)], axis=1)

    def attention(j):
        qkv[...] = dot(hid[...], wnat[j, :, :384]).astype(BF16)
        back[...] = dot(ups[...], wnat[j, :, 384:]).astype(BF16)
        for w in range(2):
            rows = slice(w * TOK, (w + 1) * TOK)
            query, key, value = (qkv[rows, kind * 128:(kind + 1) * 128] for kind in range(3))
            coming = back[rows, :]
            query_s, key_s, value_s, coming_s = (stacked(a) for a in (query, key, value, coming))
            raised = jnp.exp(dot_t(query_s, key) * SCALE) * allow
            prob = raised * (1.0 / jnp.sum(raised, axis=1, keepdims=True))
            low = prob.astype(BF16)
            mixed[j, rows, :] = dot(beside(low), value_s).astype(BF16)
            grad_prob = dot_t(coming_s, value)
            centre = jnp.sum(prob * grad_prob, axis=1, keepdims=True)
            grad_scores = (prob * (grad_prob - centre) * SCALE).astype(BF16)
            gtok[j, rows, 0:128] = dot(beside(grad_scores), key_s).astype(BF16)
            gtok[j, rows, 128:256] = t_dot(grad_scores, query_s).astype(BF16)
            gtok[j, rows, 256:384] = t_dot(low, coming_s).astype(BF16)
        grad_q = dot(hid_t[...], gtok[j]).astype(BF16)
        grad_p = dot(ups_t[...], mixed[j]).astype(BF16)
        for n in range(16):
            part = slice(n * CHUNK, (n + 1) * CHUNK)
            grad[j, natural(n), :, :384] = grad_q[part]
            grad[j, natural(n), :, 384:] = grad_p[part]

    def outputs_share(j):
        to_output = dot_t(mixed[j], wnat[j, :, 384:])
        to_hidden = dot_t(gtok[j], wnat[j, :, :384])
        if j == 0:
            opart[:, :D] = to_output
            opart[:, D:] = to_hidden
        else:
            opart[:, :D] += to_output
            opart[:, D:] += to_hidden

    def sum_start(j):
        send(line(grad, j, 2, 0, 2), h2.at[j, 0], h2_s.at[j, 0], h2_r.at[j, 0], at(0, 1))
        send(line(grad, j, 2, 2, 2), h2.at[j, 1], h2_s.at[j, 1], h2_r.at[j, 1], at(0, -1))

    def sum_relay(j):
        for side, dq in ((0, 1), (1, -1)):
            arrived(h2.at[j, side], h2_s.at[j, side], h2_r.at[j, side])
            for k in range(2):
                place = around(q, dq) * 4 + 2 * side + k
                grad[j, place] = (grad[j, place].astype(F32) + h2[j, side, k].astype(F32)).astype(BF16)
            send(line(grad, j, dq), f2.at[j, side], f2_s.at[j, side], f2_r.at[j, side], at(0, dq))

    def sum_first(j):
        for side in range(2):
            arrived(f2.at[j, side], f2_s.at[j, side], f2_r.at[j, side])
        for k in range(4):
            total = grad[j, q * 4 + k].astype(F32) + f2[j, 0, k].astype(F32) + f2[j, 1, k].astype(F32)
            psum[j, k] = total.astype(BF16)
        for d in (2, 1, 3):
            send(psum.at[j, around(p, d)], f1.at[j, d], f1_s.at[j, d], f1_r.at[j, d], at(d, 0))

    def sum_z(j):
        total = psum[j, p].astype(F32)
        for d in (1, 3, 2):
            arrived(f1.at[j, d], f1_s.at[j, d], f1_r.at[j, d])
            total = total + f1[j, d].astype(F32)
        for kind in range(4):
            for r in range(2):
                zs[j, kind * 2 + r] = total[r * 24:(r + 1) * 24, kind * 128:(kind + 1) * 128].astype(BF16)
        for d in (4, 3, 5, 2, 6, 1, 7):
            send(zs.at[j, (z + d) % 8], zr.at[j, d], z1_s.at[j, d], z1_r.at[j, d], at_z(d, chip * 2 + core))

    half_here = z % 2
    slot = (z // 2) * 2 + core
    to_sibling = []

    def hand_out(j):
        total = zs[j, z].astype(F32)
        for d in range(1, 8):
            arrived(zr.at[j, d], z1_s.at[j, d], z1_r.at[j, d])
            total = total + zr[j, d].astype(F32)
        zo[j] = total.astype(BF16)
        for d in (4, 3, 5, 2, 6, 1, 7):
            send(zo.at[j], za.at[j, slot], z2_s.at[j, d], z2_r.at[j, slot], at_z(d, chip * 2 + half_here))
        here = copy(zo.at[j], za.at[j, slot], z2_s.at[j, 0], z2_r.at[j, slot], sib)
        to_sibling.append(here)

        @pl.when(half_here == core)
        def _():
            za[j, slot] = zo[j]

        @pl.when(half_here != core)
        def _():
            here.start()

    def finish(j):
        for n in range(8):
            own = jnp.logical_and(half_here == core, slot == n)

            @pl.when(jnp.logical_not(own))
            def _():
                arrived(za.at[j, n], z2_s.at[j, 0], z2_r.at[j, n])
        for kind in range(4):
            for half in range(2):
                piece = za[j, kind * 2 + half].astype(F32)
                at_col = half * HALF + j * 128
                if kind < 3:
                    gqo_v[:, kind * D + at_col:kind * D + at_col + 128] = piece
                else:
                    gpo_v[:, at_col:at_col + 128] = piece

    gather_end(0)
    attention(0)
    sum_start(0)
    gather_relay(2)
    outputs_share(0)
    gather_end(1)
    attention(1)
    sum_start(1)
    sum_relay(0)
    outputs_share(1)
    gather_end(2)
    attention(2)
    sum_start(2)
    outputs_share(2)
    xs[...] = opart[their_rows, :].astype(BF16)
    send(xs, xr, par_s, par_r, sib)
    sum_relay(1)
    sum_first(0)

    arrived(xr, par_s, par_r)
    total = win[:, :D].astype(F32) + opart[my_rows, :D] + xr[:, :D].astype(F32)
    rsend[:, :D] = total.astype(BF16)
    grad_hidden = opart[my_rows, D:] + xr[:, D:].astype(F32)
    normalized = norm[...]
    centre = jnp.mean(grad_hidden, axis=1, keepdims=True)
    along_norm = jnp.mean(grad_hidden * normalized, axis=1, keepdims=True)
    moved = (grad_hidden - centre - normalized * along_norm) * inv_ref[:, :1]
    rsend[:, D:] = (win[:, D:].astype(F32) + moved).astype(BF16)
    for group in range(4):
        for level, dz in ((1, -1), (0, 1)):
            n = level * 4 + group
            send(rsend.at[span(1 - level, group)], rrecv.at[span(level, group)], ret_s.at[n], ret_r.at[n],
                 near(dz, BACK[group]))

    sum_relay(2)
    sum_first(1)
    sum_z(0)
    sum_first(2)
    sum_z(1)
    hand_out(0)
    sum_z(2)
    hand_out(1)

    for n in range(8):
        arrived(rrecv.at[pl.ds(n * 16, 16)], ret_s.at[n], ret_r.at[n])
    order_t = (rows_i == block_source(cols_i, flag)).astype(F32).astype(BF16)
    out_v[...] = dot(order_t, rrecv[:, :D]).astype(BF16)
    gt_v[...] = dot(order_t, rrecv[:, D:]).astype(BF16)
    written = [
        pltpu.make_async_copy(a, b, out_sem.at[i])
        for i, (a, b) in enumerate(((out_v, out_hbm), (gt_v, gt_hbm), (gqo_v, gqo_hbm), (gpo_v, gpo_hbm)))
    ]
    written[0].start()
    written[1].start()
    hand_out(2)
    finish(0)
    finish(1)
    finish(2)
    written[2].start()
    written[3].start()
    for c in started:
        c.wait_send()

    @pl.when(half_here != core)
    def _():
        for c in to_sibling:
            c.wait_send()

    for c in written:
        c.wait()


def place_body(*refs):
    ins, outs, held, sem = refs[:4], refs[4:8], refs[8:12], refs[12]
    reads = [pltpu.make_async_copy(a, b, sem.at[0, i]) for i, (a, b) in enumerate(zip(ins, held))]
    writes = [pltpu.make_async_copy(a, b, sem.at[1, i]) for i, (a, b) in enumerate(zip(held, outs))]
    for c in reads:
        c.start()
    for r, w in zip(reads, writes):
        r.wait()
        w.start()
    for c in writes:
        c.wait()


def shards(tokens, w_qkv, w_proj, seam_codes, upstream):
    dma = pltpu.SemaphoreType.DMA
    vmem = pltpu.VMEM
    scratch = [
        vmem((TOK, D), BF16),
        vmem((TOK, D), BF16),
        vmem((24, 3 * D), BF16),
        vmem((24, D), BF16),
        pltpu.SMEM((2, 32), jnp.int32),
        vmem((TOK, 2 * D), BF16),
        vmem((TOK, 2 * D), BF16),
        vmem((2, 24, COLS), BF16),
        vmem((24, COLS), BF16),
        vmem((GROUPS, 16, CHUNK, WIDE), BF16),
        vmem((GROUPS, D, WIDE), BF16),
        vmem((2 * TOK, D), BF16),
        vmem((2 * TOK, D), BF16),
        vmem((D, 2 * TOK), BF16),
        vmem((D, 2 * TOK), BF16),
        vmem((TOK, D), F32),
        vmem((TOK, 128), F32),
        vmem((2 * TOK, 384), BF16),
        vmem((2 * TOK, 128), BF16),
        vmem((GROUPS, 2 * TOK, 128), BF16),
        vmem((GROUPS, 2 * TOK, 384), BF16),
        vmem((2 * TOK, 2 * D), F32),
        vmem((TOK, 2 * D), BF16),
        vmem((TOK, 2 * D), BF16),
        vmem((TOK, 2 * D), BF16),
        vmem((TOK, 2 * D), BF16),
        vmem((GROUPS, 16, CHUNK, WIDE), BF16),
        vmem((GROUPS, 2, 2, CHUNK, WIDE), BF16),
        vmem((GROUPS, 2, 4, CHUNK, WIDE), BF16),
        vmem((GROUPS, 4, CHUNK, WIDE), BF16),
        vmem((GROUPS, 4, CHUNK, WIDE), BF16),
        vmem((GROUPS, 8, 24, 128), BF16),
        vmem((GROUPS, 8, 24, 128), BF16),
        vmem((GROUPS, 24, 128), BF16),
        vmem((GROUPS, 8, 24, 128), BF16),
        vmem((TOK, D), BF16),
        vmem((TOK, D), BF16),
        vmem((24, 3 * D), F32),
        vmem((24, D), F32),
        dma((5,)), dma((4,)),
        dma((8,)), dma((8,)),
        dma, dma,
        dma((GROUPS, 4)), dma((GROUPS, 4)),
        dma((GROUPS, 4)), dma((GROUPS, 4)),
        dma((2,)), dma((2,)),
        dma, dma,
        dma((8,)), dma((8,)),
        dma((GROUPS, 2)), dma((GROUPS, 2)),
        dma((GROUPS, 2)), dma((GROUPS, 2)),
        dma((GROUPS, 4)), dma((GROUPS, 4)),
        dma((GROUPS, 8)), dma((GROUPS, 8)), dma((GROUPS, 8)), dma((GROUPS, 8)),
    ]
    anywhere = pl.BlockSpec(memory_space=pl.ANY)
    shapes = (
        jax.ShapeDtypeStruct((TOK, D), BF16),
        jax.ShapeDtypeStruct((TOK, D), BF16),
        jax.ShapeDtypeStruct((24, 3 * D), F32),
        jax.ShapeDtypeStruct((24, D), F32),
    )
    results = pl.pallas_call(
        body,
        out_shape=shapes,
        in_specs=[anywhere] * 5,
        out_specs=(anywhere,) * 4,
        scratch_shapes=scratch,
        compiler_params=pltpu.CompilerParams(
            collective_id=0, has_side_effects=True, vmem_limit_bytes=56 * 1024 * 1024
        ),
        name="layer",
    )(tokens.reshape(TOK, D), upstream.reshape(TOK, D), w_qkv, w_proj, seam_codes.T)
    out, grad_tok, grad_qkv, grad_proj = pl.pallas_call(
        place_body,
        out_shape=shapes,
        in_specs=[anywhere] * 4,
        out_specs=(anywhere,) * 4,
        scratch_shapes=[vmem(a.shape, a.dtype) for a in shapes] + [dma((2, 4))],
        name="place",
    )(*results)
    return (out.reshape(tokens.shape), grad_tok.reshape(tokens.shape), grad_qkv, grad_proj)


def solution(mesh):
    field = P("rep", "lev", "tile", None, None, None)
    rows = P("tile", None)
    return jax.shard_map(
        shards,
        mesh=mesh,
        in_specs=(field, rows, rows, P(), field),
        out_specs=(field, field, rows, rows),
        check_vma=False,
    )
```

time: 77 us -> 73 us (0.948)
  local copies, waits for them, and re-layouts: 6.95 us -> 0 us
  Pallas kernels: 68.6 us -> 72.2 us
    unnamed x15 -> x0, local copies, waits for them, and re-layouts: 6.95 us -> none
    pallas_call x1 -> x2, Pallas kernels: 68.6 us -> 72.2 us  [the longest x1 70.3 us: shards(): pl.pallas_call(body, out_shape=shapes, in_specs=[anywhere] * 5, out_specs...]
where the time goes in v2:
time: 73 us; the launch traced here: 72.8 us
  Pallas kernels  72.2 us (99%)
    pallas_call x1, Pallas kernels, shards(): pl.pallas_call(body, out_shape=shapes, in_specs=[anywhere] * 5, out_specs...  70.3 us
    pallas_call x1, Pallas kernels, shards(): pl.pallas_call(place_body, out_shape=shapes, in_specs=[anywhere] * 4, out...  1.9 us

profile of v2, /device:TPU:1, one launch (start us, length us, event | category | flops | bytes accessed | tf_op | source)
XLA Modules:
  0.0 72.8 jit_solution(1536454661102646972)
XLA Ops:
  0.6 70.3 %layer.1 = (bf16[128,768]{1,0:T(8,128)(2,1)}, bf16[128,768]{1,0:T(8,128)(2,1)}, f32[24,2304]{1,0:T(8,128)}, f32[24,768]{1,0:T(8,128)}) custom-call(bf16[128,768]{1,0:T(8,128)(2,1)} %bitcast.9, bf16[128,768]{1,0:T(8,128)(2,1)} %bitcast.10, bf16[24,2304]{1,0:T(8,128)(2,1)} %wq_hbm.1, bf16[24,768]{1,0:T(8,128)(2,1)} %wp_hbm.1, s32[2,32]{1,0:T(2,128)} %bitcast.11), custom_call_target="tpu_custom_call" | custom-call | tf_op jit(solution)/shard_map/layer/pallas_call | solution.py:475
  70.9 1.9 %place.1 = (bf16[128,768]{1,0:T(8,128)(2,1)}, bf16[128,768]{1,0:T(8,128)(2,1)}, f32[24,2304]{1,0:T(8,128)}, f32[24,768]{1,0:T(8,128)}) custom-call(bf16[128,768]{1,0:T(8,128)(2,1)} %get-tuple-element.12.refs_0_, bf16[128,768]{1,0:T(8,128)(2,1)} %get-tuple-element.13.refs_1_, f32[24,2304]{1,0:T(8,128)} %get-tuple-element.14.refs_2_, ...), custom_call_target="tpu_custom_call" | custom-call | tf_op jit(solution)/shard_map/place/pallas_call | solution.py:486

commit v3 on v2

--- a/solution.py
+++ b/solution.py
@@ -17,6 +17,9 @@
 COLS = 4 * HALF
 GROUPS = 3
 WIDE = COLS // GROUPS
+ALONG = (2, 1, -1, 0)
+SUM_UP = (0,)
+DIRECT_OUT = ()
 CHUNK = 48
 TOK = 128
 
@@ -154,6 +157,9 @@
     def line(buf, j, dq, start=0, count=4):
         return buf.at[j, pl.ds(around(q, dq) * 4 + start, count)]
 
+    def cell(buf, j, dp, dq):
+        return buf.at[j, around(q, dq) * 4 + around(p, dp)]
+
     def gather_first(j):
         own = wbuf.at[j, q * 4 + p]
         for d in (1, 3, 2):
@@ -201,6 +207,7 @@
     hid[my_rows, :] = normalized.astype(BF16)
     send(hid.at[my_rows], hid.at[my_rows], sib_s.at[0], sib_r.at[0], sib)
     gather_relay(1)
+    gather_relay(2)
     arrived(ups.at[their_rows], sib_s.at[1], sib_r.at[1])
     arrived(hid.at[their_rows], sib_s.at[0], sib_r.at[0])
     hid_t[...] = hid[...].T
@@ -218,9 +225,11 @@
     def beside(part):
         return jnp.concatenate([part[h * TOK:(h + 1) * TOK] for h in range(4)], axis=1)
 
-    def attention(j):
+    def project(j):
         qkv[...] = dot(hid[...], wnat[j, :, :384]).astype(BF16)
         back[...] = dot(ups[...], wnat[j, :, 384:]).astype(BF16)
+
+    def attend(j):
         for w in range(2):
             rows = slice(w * TOK, (w + 1) * TOK)
             query, key, value = (qkv[rows, kind * 128:(kind + 1) * 128] for kind in range(3))
@@ -236,6 +245,8 @@
             gtok[j, rows, 0:128] = dot(beside(grad_scores), key_s).astype(BF16)
             gtok[j, rows, 128:256] = t_dot(grad_scores, query_s).astype(BF16)
             gtok[j, rows, 256:384] = t_dot(low, coming_s).astype(BF16)
+
+    def weight_grads(j):
         grad_q = dot(hid_t[...], gtok[j]).astype(BF16)
         grad_p = dot(ups_t[...], mixed[j]).astype(BF16)
         for n in range(16):
@@ -253,29 +264,45 @@
             opart[:, :D] += to_output
             opart[:, D:] += to_hidden
 
+    def sum_way(j, k, way, dq):
+        send(cell(grad, j, ALONG[k], dq), f2.at[j, way, k], f2_s.at[j, way, k], f2_r.at[j, way, k], at(0, dq))
+
     def sum_start(j):
-        send(line(grad, j, 2, 0, 2), h2.at[j, 0], h2_s.at[j, 0], h2_r.at[j, 0], at(0, 1))
-        send(line(grad, j, 2, 2, 2), h2.at[j, 1], h2_s.at[j, 1], h2_r.at[j, 1], at(0, -1))
+        for k in range(4):
+            if j in DIRECT_OUT:
+                for way, dq in ((2, 2), (0, 1), (1, -1)):
+                    sum_way(j, k, way, dq)
+            else:
+                dq = 1 if k in SUM_UP else -1
+                send(cell(grad, j, ALONG[k], 2), h2.at[j, k], h2_s.at[j, k], h2_r.at[j, k], at(0, dq))
+        if j not in DIRECT_OUT:
+            for k in range(4):
+                way, dq = (1, -1) if k in SUM_UP else (0, 1)
+                sum_way(j, k, way, dq)
 
     def sum_relay(j):
-        for side, dq in ((0, 1), (1, -1)):
-            arrived(h2.at[j, side], h2_s.at[j, side], h2_r.at[j, side])
-            for k in range(2):
-                place = around(q, dq) * 4 + 2 * side + k
-                grad[j, place] = (grad[j, place].astype(F32) + h2[j, side, k].astype(F32)).astype(BF16)
-            send(line(grad, j, dq), f2.at[j, side], f2_s.at[j, side], f2_r.at[j, side], at(0, dq))
+        if j in DIRECT_OUT:
+            return
+        for k in range(4):
+            way, dq = (0, 1) if k in SUM_UP else (1, -1)
+            arrived(h2.at[j, k], h2_s.at[j, k], h2_r.at[j, k])
+            place = around(q, dq) * 4 + around(p, ALONG[k])
+            grad[j, place] = (grad[j, place].astype(F32) + h2[j, k].astype(F32)).astype(BF16)
+            sum_way(j, k, way, dq)
 
     def sum_first(j):
-        for side in range(2):
-            arrived(f2.at[j, side], f2_s.at[j, side], f2_r.at[j, side])
         for k in range(4):
-            total = grad[j, q * 4 + k].astype(F32) + f2[j, 0, k].astype(F32) + f2[j, 1, k].astype(F32)
+            total = grad[j, q * 4 + around(p, ALONG[k])].astype(F32)
+            for way in (0, 1, 2) if j in DIRECT_OUT else (0, 1):
+                arrived(f2.at[j, way, k], f2_s.at[j, way, k], f2_r.at[j, way, k])
+                total = total + f2[j, way, k].astype(F32)
             psum[j, k] = total.astype(BF16)
-        for d in (2, 1, 3):
-            send(psum.at[j, around(p, d)], f1.at[j, d], f1_s.at[j, d], f1_r.at[j, d], at(d, 0))
+            if k < 3:
+                d = (2, 1, 3)[k]
+                send(psum.at[j, k], f1.at[j, d], f1_s.at[j, d], f1_r.at[j, d], at(d, 0))
 
     def sum_z(j):
-        total = psum[j, p].astype(F32)
+        total = psum[j, 3].astype(F32)
         for d in (1, 3, 2):
             arrived(f1.at[j, d], f1_s.at[j, d], f1_r.at[j, d])
             total = total + f1[j, d].astype(F32)
@@ -324,46 +351,52 @@
                 else:
                     gpo_v[:, at_col:at_col + 128] = piece
 
+    def give_back():
+        arrived(xr, par_s, par_r)
+        total = win[:, :D].astype(F32) + opart[my_rows, :D] + xr[:, :D].astype(F32)
+        rsend[:, :D] = total.astype(BF16)
+        grad_hidden = opart[my_rows, D:] + xr[:, D:].astype(F32)
+        normalized = norm[...]
+        centre = jnp.mean(grad_hidden, axis=1, keepdims=True)
+        along_norm = jnp.mean(grad_hidden * normalized, axis=1, keepdims=True)
+        moved = (grad_hidden - centre - normalized * along_norm) * inv_ref[:, :1]
+        rsend[:, D:] = (win[:, D:].astype(F32) + moved).astype(BF16)
+        for group in range(4):
+            for level, dz in ((1, -1), (0, 1)):
+                n = level * 4 + group
+                send(rsend.at[span(1 - level, group)], rrecv.at[span(level, group)], ret_s.at[n], ret_r.at[n],
+                     near(dz, BACK[group]))
+
     gather_end(0)
-    attention(0)
+    project(0)
+    attend(0)
+    weight_grads(0)
     sum_start(0)
-    gather_relay(2)
-    outputs_share(0)
     gather_end(1)
-    attention(1)
+    project(1)
+    attend(1)
+    weight_grads(1)
     sum_start(1)
     sum_relay(0)
+    gather_end(2)
+    project(2)
+    attend(2)
+    weight_grads(2)
+    sum_start(2)
+    outputs_share(0)
     outputs_share(1)
-    gather_end(2)
-    attention(2)
-    sum_start(2)
     outputs_share(2)
     xs[...] = opart[their_rows, :].astype(BF16)
     send(xs, xr, par_s, par_r, sib)
     sum_relay(1)
     sum_first(0)
-
-    arrived(xr, par_s, par_r)
-    total = win[:, :D].astype(F32) + opart[my_rows, :D] + xr[:, :D].astype(F32)
-    rsend[:, :D] = total.astype(BF16)
-    grad_hidden = opart[my_rows, D:] + xr[:, D:].astype(F32)
-    normalized = norm[...]
-    centre = jnp.mean(grad_hidden, axis=1, keepdims=True)
-    along_norm = jnp.mean(grad_hidden * normalized, axis=1, keepdims=True)
-    moved = (grad_hidden - centre - normalized * along_norm) * inv_ref[:, :1]
-    rsend[:, D:] = (win[:, D:].astype(F32) + moved).astype(BF16)
-    for group in range(4):
-        for level, dz in ((1, -1), (0, 1)):
-            n = level * 4 + group
-            send(rsend.at[span(1 - level, group)], rrecv.at[span(level, group)], ret_s.at[n], ret_r.at[n],
-                 near(dz, BACK[group]))
-
     sum_relay(2)
+    give_back()
+    sum_z(0)
     sum_first(1)
-    sum_z(0)
     sum_first(2)
+    hand_out(0)
     sum_z(1)
-    hand_out(0)
     sum_z(2)
     hand_out(1)
 
@@ -378,8 +411,8 @@
     ]
     written[0].start()
     written[1].start()
+    finish(0)
     hand_out(2)
-    finish(0)
     finish(1)
     finish(2)
     written[2].start()
@@ -440,8 +473,8 @@
         vmem((TOK, 2 * D), BF16),
         vmem((TOK, 2 * D), BF16),
         vmem((GROUPS, 16, CHUNK, WIDE), BF16),
-        vmem((GROUPS, 2, 2, CHUNK, WIDE), BF16),
-        vmem((GROUPS, 2, 4, CHUNK, WIDE), BF16),
+        vmem((GROUPS, 4, CHUNK, WIDE), BF16),
+        vmem((GROUPS, 3, 4, CHUNK, WIDE), BF16),
         vmem((GROUPS, 4, CHUNK, WIDE), BF16),
         vmem((GROUPS, 4, CHUNK, WIDE), BF16),
         vmem((GROUPS, 8, 24, 128), BF16),
@@ -460,8 +493,8 @@
         dma((2,)), dma((2,)),
         dma, dma,
         dma((8,)), dma((8,)),
-        dma((GROUPS, 2)), dma((GROUPS, 2)),
-        dma((GROUPS, 2)), dma((GROUPS, 2)),
+        dma((GROUPS, 4)), dma((GROUPS, 4)),
+        dma((GROUPS, 3, 4)), dma((GROUPS, 3, 4)),
         dma((GROUPS, 4)), dma((GROUPS, 4)),
         dma((GROUPS, 8)), dma((GROUPS, 8)), dma((GROUPS, 8)), dma((GROUPS, 8)),
     ]

time: 73 us -> 67.1 us (0.919)
  Pallas kernels: 72.2 us -> 66.4 us
    pallas_call x1, Pallas kernels: 70.3 us -> 64.5 us  [shards(): pl.pallas_call(body, out_shape=shapes, in_specs=[anywhere] * 5, out_specs...]
where the time goes in v3:
time: 67.1 us; the launch traced here: 67 us
  Pallas kernels  66.4 us (99%)
    pallas_call x1, Pallas kernels, shards(): pl.pallas_call(body, out_shape=shapes, in_specs=[anywhere] * 5, out_specs...  64.5 us
    pallas_call x1, Pallas kernels, shards(): pl.pallas_call(place_body, out_shape=shapes, in_specs=[anywhere] * 4, out...  1.9 us

profile of v3, /device:TPU:1, one launch (start us, length us, event | category | flops | bytes accessed | tf_op | source)
XLA Modules:
  0.0 67.0 jit_solution(10399858946430296668)
XLA Ops:
  0.6 64.5 %layer.1 = (bf16[128,768]{1,0:T(8,128)(2,1)}, bf16[128,768]{1,0:T(8,128)(2,1)}, f32[24,2304]{1,0:T(8,128)}, f32[24,768]{1,0:T(8,128)}) custom-call(bf16[128,768]{1,0:T(8,128)(2,1)} %bitcast.9, bf16[128,768]{1,0:T(8,128)(2,1)} %bitcast.10, bf16[24,2304]{1,0:T(8,128)(2,1)} %wq_hbm.1, bf16[24,768]{1,0:T(8,128)(2,1)} %wp_hbm.1, s32[2,32]{1,0:T(2,128)} %bitcast.11), custom_call_target="tpu_custom_call" | custom-call | tf_op jit(solution)/shard_map/layer/pallas_call | solution.py:508
  65.1 1.9 %place.1 = (bf16[128,768]{1,0:T(8,128)(2,1)}, bf16[128,768]{1,0:T(8,128)(2,1)}, f32[24,2304]{1,0:T(8,128)}, f32[24,768]{1,0:T(8,128)}) custom-call(bf16[128,768]{1,0:T(8,128)(2,1)} %get-tuple-element.12.refs_0_, bf16[128,768]{1,0:T(8,128)(2,1)} %get-tuple-element.13.refs_1_, f32[24,2304]{1,0:T(8,128)} %get-tuple-element.14.refs_2_, ...), custom_call_target="tpu_custom_call" | custom-call | tf_op jit(solution)/shard_map/place/pallas_call | solution.py:519

commit v4 on v3

--- a/solution.py
+++ b/solution.py
@@ -50,11 +50,11 @@
 
 def body(
     tok_hbm, upi_hbm, wq_hbm, wp_hbm, codes_hbm,
-    out_hbm, gt_hbm, gqo_hbm, gpo_hbm,
-    tok, upi, wq, wp, codes, blocks, win, stage, wsib, wbuf, wnat, hid, ups, hid_t, ups_t, norm, inv_ref,
-    qkv, back, mixed, gtok, opart, xs, xr, rsend, rrecv, grad, h2, f2, psum, f1, zs, zr, zo, za,
-    out_v, gt_v, gqo_v, gpo_v,
-    in_sem, out_sem,
+    out_hbm, gt_hbm, za,
+    tok, upi, wq, wp, codes, blocks, win, stage, wout, wsib, wbuf, wnat, hid, ups, hid_t, ups_t, norm, inv_ref,
+    qkv, back, mixed, gtok, opart, xs, xr, rsend, rrecv, grad, h2, f2, psum, f1, zs, zr, zo,
+    out_v, gt_v,
+    in_sem, out_sem, own_sem,
     roll_s, roll_r, w_s, w_r, ga_s, ga_r, gb_s, gb_r, sib_s, sib_r, par_s, par_r, ret_s, ret_r,
     h2_s, h2_r, f2_s, f2_r, f1_s, f1_r, z1_s, z1_r, z2_s, z2_r,
 ):
@@ -132,9 +132,11 @@
     order = (cols_i == block_source(rows_i, flag)).astype(F32).astype(BF16)
     blocks[:, :D] = dot(order, tok[...]).astype(BF16)
     blocks[:, D:] = dot(order, upi[...]).astype(BF16)
+    leaving = stage[1 - core].astype(F32)
+    wout[...] = jnp.concatenate([leaving[:, :D], leaving[:, D:]], axis=0).astype(BF16)
     pl.semaphore_wait(barrier, len(partners))
 
-    send(stage.at[1 - core], wsib, w_s, w_r, sib)
+    send(wout, wsib, w_s, w_r, sib)
 
     def span(level, group):
         return pl.ds(level * 64 + group * 16, 16)
@@ -148,6 +150,7 @@
     arrived(wsib, w_s, w_r)
     mine = stage[core].astype(F32)
     other = wsib[...].astype(F32)
+    other = jnp.concatenate([other[:24], other[24:]], axis=1)
     first = jnp.where(core == 0, mine, other)
     second = jnp.where(core == 0, other, mine)
     chunk = jnp.concatenate([first, second], axis=0).astype(BF16)
@@ -173,16 +176,16 @@
 
     def gather_relay(j):
         arrived(line(wbuf, j, -1), gb_s.at[j, 0], gb_r.at[j, 0])
-        send(line(wbuf, j, -1, 0, 2), line(wbuf, j, -1, 0, 2), gb_s.at[j, 2], gb_r.at[j, 2], at(0, 1))
+        send(line(wbuf, j, -1, 0, 3), line(wbuf, j, -1, 0, 3), gb_s.at[j, 2], gb_r.at[j, 2], at(0, 1))
         arrived(line(wbuf, j, 1), gb_s.at[j, 1], gb_r.at[j, 1])
-        send(line(wbuf, j, 1, 2, 2), line(wbuf, j, 1, 2, 2), gb_s.at[j, 3], gb_r.at[j, 3], at(0, -1))
+        send(line(wbuf, j, 1, 3, 1), line(wbuf, j, 1, 3, 1), gb_s.at[j, 3], gb_r.at[j, 3], at(0, -1))
 
     def natural(n):
         return n + core * ((n % 4) * 4 + n // 4 - n)
 
     def gather_end(j):
-        arrived(line(wbuf, j, 2, 0, 2), gb_s.at[j, 2], gb_r.at[j, 2])
-        arrived(line(wbuf, j, 2, 2, 2), gb_s.at[j, 3], gb_r.at[j, 3])
+        arrived(line(wbuf, j, 2, 0, 3), gb_s.at[j, 2], gb_r.at[j, 2])
+        arrived(line(wbuf, j, 2, 3, 1), gb_s.at[j, 3], gb_r.at[j, 3])
         for n in range(16):
             wnat[j, n * CHUNK:(n + 1) * CHUNK, :] = wbuf[j, natural(n)]
 
@@ -329,7 +332,7 @@
 
         @pl.when(half_here == core)
         def _():
-            za[j, slot] = zo[j]
+            pltpu.make_async_copy(zo.at[j], za.at[j, slot], own_sem.at[j]).start()
 
         @pl.when(half_here != core)
         def _():
@@ -342,14 +345,10 @@
             @pl.when(jnp.logical_not(own))
             def _():
                 arrived(za.at[j, n], z2_s.at[j, 0], z2_r.at[j, n])
-        for kind in range(4):
-            for half in range(2):
-                piece = za[j, kind * 2 + half].astype(F32)
-                at_col = half * HALF + j * 128
-                if kind < 3:
-                    gqo_v[:, kind * D + at_col:kind * D + at_col + 128] = piece
-                else:
-                    gpo_v[:, at_col:at_col + 128] = piece
+
+        @pl.when(half_here == core)
+        def _():
+            pltpu.make_async_copy(zo.at[j], za.at[j, slot], own_sem.at[j]).wait()
 
     def give_back():
         arrived(xr, par_s, par_r)
@@ -384,11 +383,11 @@
     weight_grads(2)
     sum_start(2)
     outputs_share(0)
+    sum_relay(1)
     outputs_share(1)
     outputs_share(2)
     xs[...] = opart[their_rows, :].astype(BF16)
     send(xs, xr, par_s, par_r, sib)
-    sum_relay(1)
     sum_first(0)
     sum_relay(2)
     give_back()
@@ -407,7 +406,7 @@
     gt_v[...] = dot(order_t, rrecv[:, D:]).astype(BF16)
     written = [
         pltpu.make_async_copy(a, b, out_sem.at[i])
-        for i, (a, b) in enumerate(((out_v, out_hbm), (gt_v, gt_hbm), (gqo_v, gqo_hbm), (gpo_v, gpo_hbm)))
+        for i, (a, b) in enumerate(((out_v, out_hbm), (gt_v, gt_hbm)))
     ]
     written[0].start()
     written[1].start()
@@ -415,8 +414,6 @@
     hand_out(2)
     finish(1)
     finish(2)
-    written[2].start()
-    written[3].start()
     for c in started:
         c.wait_send()
 
@@ -429,15 +426,31 @@
         c.wait()
 
 
-def place_body(*refs):
-    ins, outs, held, sem = refs[:4], refs[4:8], refs[8:12], refs[12]
-    reads = [pltpu.make_async_copy(a, b, sem.at[0, i]) for i, (a, b) in enumerate(zip(ins, held))]
-    writes = [pltpu.make_async_copy(a, b, sem.at[1, i]) for i, (a, b) in enumerate(zip(held, outs))]
+def place_body(out_a, gt_a, za_a, out_b, gt_b, gq_b, gp_b, out_v, gt_v, za_v, gq_v, gp_v, sem):
+    reads = [
+        pltpu.make_async_copy(a, b, sem.at[0, i]) for i, (a, b) in enumerate(((za_a, za_v), (out_a, out_v), (gt_a, gt_v)))
+    ]
+    writes = [
+        pltpu.make_async_copy(a, b, sem.at[1, i])
+        for i, (a, b) in enumerate(((gq_v, gq_b), (gp_v, gp_b), (out_v, out_b), (gt_v, gt_b)))
+    ]
     for c in reads:
         c.start()
-    for r, w in zip(reads, writes):
-        r.wait()
-        w.start()
+    reads[0].wait()
+    for kind in range(4):
+        for j in range(GROUPS):
+            for half in range(2):
+                piece = za_v[j, kind * 2 + half].astype(F32)
+                at_col = half * HALF + j * 128
+                if kind < 3:
+                    gq_v[:, kind * D + at_col:kind * D + at_col + 128] = piece
+                else:
+                    gp_v[:, at_col:at_col + 128] = piece
+    writes[0].start()
+    writes[1].start()
+    for k in (1, 2):
+        reads[k].wait()
+        writes[k + 1].start()
     for c in writes:
         c.wait()
 
@@ -454,7 +467,8 @@
         vmem((TOK, 2 * D), BF16),
         vmem((TOK, 2 * D), BF16),
         vmem((2, 24, COLS), BF16),
-        vmem((24, COLS), BF16),
+        vmem((48, D), BF16),
+        vmem((48, D), BF16),
         vmem((GROUPS, 16, CHUNK, WIDE), BF16),
         vmem((GROUPS, D, WIDE), BF16),
         vmem((2 * TOK, D), BF16),
@@ -480,12 +494,9 @@
         vmem((GROUPS, 8, 24, 128), BF16),
         vmem((GROUPS, 8, 24, 128), BF16),
         vmem((GROUPS, 24, 128), BF16),
-        vmem((GROUPS, 8, 24, 128), BF16),
         vmem((TOK, D), BF16),
         vmem((TOK, D), BF16),
-        vmem((24, 3 * D), F32),
-        vmem((24, D), F32),
-        dma((5,)), dma((4,)),
+        dma((5,)), dma((2,)), dma((GROUPS,)),
         dma((8,)), dma((8,)),
         dma, dma,
         dma((GROUPS, 4)), dma((GROUPS, 4)),
@@ -505,11 +516,12 @@
         jax.ShapeDtypeStruct((24, 3 * D), F32),
         jax.ShapeDtypeStruct((24, D), F32),
     )
+    pieces = jax.ShapeDtypeStruct((GROUPS, 8, 24, 128), BF16)
     results = pl.pallas_call(
         body,
-        out_shape=shapes,
+        out_shape=shapes[:2] + (pieces,),
         in_specs=[anywhere] * 5,
-        out_specs=(anywhere,) * 4,
+        out_specs=(anywhere,) * 3,
         scratch_shapes=scratch,
         compiler_params=pltpu.CompilerParams(
             collective_id=0, has_side_effects=True, vmem_limit_bytes=56 * 1024 * 1024
@@ -519,9 +531,9 @@
     out, grad_tok, grad_qkv, grad_proj = pl.pallas_call(
         place_body,
         out_shape=shapes,
-        in_specs=[anywhere] * 4,
+        in_specs=[anywhere] * 3,
         out_specs=(anywhere,) * 4,
-        scratch_shapes=[vmem(a.shape, a.dtype) for a in shapes] + [dma((2, 4))],
+        scratch_shapes=[vmem(a.shape, a.dtype) for a in shapes[:2] + (pieces,) + shapes[2:]] + [dma((2, 4))],
         name="place",
     )(*results)
     return (out.reshape(tokens.shape), grad_tok.reshape(tokens.shape), grad_qkv, grad_proj)

time: 67.1 us -> 66.3 us (0.988)
  Pallas kernels: 66.4 us -> 65.5 us
    pallas_call x2, Pallas kernels: 66.4 us -> 65.5 us  [the longest x1 63.7 us: shards(): pl.pallas_call(body, out_shape=shapes[:2] + (pieces,), in_specs=[anywhere...]
where the time goes in v4:
time: 66.3 us; the launch traced here: 66.1 us
  Pallas kernels  65.5 us (99%)
    pallas_call x1, Pallas kernels, shards(): pl.pallas_call(body, out_shape=shapes[:2] + (pieces,), in_specs=[anywhere...  63.7 us
    pallas_call x1, Pallas kernels, shards(): pl.pallas_call(place_body, out_shape=shapes, in_specs=[anywhere] * 3, out...  1.84 us

profile of v4, /device:TPU:1, one launch (start us, length us, event | category | flops | bytes accessed | tf_op | source)
XLA Modules:
  0.0 66.1 jit_solution(13900957118137181761)
XLA Ops:
  0.6 63.7 %layer.1 = (bf16[128,768]{1,0:T(8,128)(2,1)}, bf16[128,768]{1,0:T(8,128)(2,1)}, bf16[3,8,24,128]{3,2,1,0:T(8,128)(2,1)}) custom-call(bf16[128,768]{1,0:T(8,128)(2,1)} %bitcast.9, bf16[128,768]{1,0:T(8,128)(2,1)} %bitcast.10, bf16[24,2304]{1,0:T(8,128)(2,1)} %wq_hbm.1, bf16[24,768]{1,0:T(8,128)(2,1)} %wp_hbm.1, s32[2,32]{1,0:T(2,128)} %bitcast.11), custom_call_target="tpu_custom_call" | custom-call | tf_op jit(solution)/shard_map/layer/pallas_call | solution.py:520
  64.3 1.8 %place.1 = (bf16[128,768]{1,0:T(8,128)(2,1)}, bf16[128,768]{1,0:T(8,128)(2,1)}, f32[24,2304]{1,0:T(8,128)}, f32[24,768]{1,0:T(8,128)}) custom-call(bf16[128,768]{1,0:T(8,128)(2,1)} %get-tuple-element.11.out_a, bf16[128,768]{1,0:T(8,128)(2,1)} %get-tuple-element.12.gt_a, bf16[3,8,24,128]{3,2,1,0:T(8,128)(2,1)} %get-tuple-element.13.za_a), custom_call_target="tpu_custom_call" | custom-call | tf_op jit(solution)/shard_map/place/pallas_call | solution.py:531

commit v5 on v4

--- a/solution.py
+++ b/solution.py
@@ -376,9 +376,9 @@
     attend(1)
     weight_grads(1)
     sum_start(1)
-    sum_relay(0)
     gather_end(2)
     project(2)
+    sum_relay(0)
     attend(2)
     weight_grads(2)
     sum_start(2)
@@ -397,7 +397,6 @@
     hand_out(0)
     sum_z(1)
     sum_z(2)
-    hand_out(1)
 
     for n in range(8):
         arrived(rrecv.at[pl.ds(n * 16, 16)], ret_s.at[n], ret_r.at[n])
@@ -410,8 +409,9 @@
     ]
     written[0].start()
     written[1].start()
+    hand_out(1)
+    hand_out(2)
     finish(0)
-    hand_out(2)
     finish(1)
     finish(2)
     for c in started:

time: 66.3 us -> 66.2 us (level)
  no operation moved by 1% of the time
where the time goes in v5:
time: 66.2 us; the launch traced here: 66 us
  Pallas kernels  65.4 us (99%)
    pallas_call x1, Pallas kernels, shards(): pl.pallas_call(body, out_shape=shapes[:2] + (pieces,), in_specs=[anywhere...  63.6 us
    pallas_call x1, Pallas kernels, shards(): pl.pallas_call(place_body, out_shape=shapes, in_specs=[anywhere] * 3, out...  1.84 us

profile of v5, /device:TPU:1, one launch (start us, length us, event | category | flops | bytes accessed | tf_op | source)
XLA Modules:
  0.0 66.0 jit_solution(16160228627505564566)
XLA Ops:
  0.6 63.6 %layer.1 = (bf16[128,768]{1,0:T(8,128)(2,1)}, bf16[128,768]{1,0:T(8,128)(2,1)}, bf16[3,8,24,128]{3,2,1,0:T(8,128)(2,1)}) custom-call(bf16[128,768]{1,0:T(8,128)(2,1)} %bitcast.9, bf16[128,768]{1,0:T(8,128)(2,1)} %bitcast.10, bf16[24,2304]{1,0:T(8,128)(2,1)} %wq_hbm.1, bf16[24,768]{1,0:T(8,128)(2,1)} %wp_hbm.1, s32[2,32]{1,0:T(2,128)} %bitcast.11), custom_call_target="tpu_custom_call" | custom-call | tf_op jit(solution)/shard_map/layer/pallas_call | solution.py:520
  64.2 1.8 %place.1 = (bf16[128,768]{1,0:T(8,128)(2,1)}, bf16[128,768]{1,0:T(8,128)(2,1)}, f32[24,2304]{1,0:T(8,128)}, f32[24,768]{1,0:T(8,128)}) custom-call(bf16[128,768]{1,0:T(8,128)(2,1)} %get-tuple-element.11.out_a, bf16[128,768]{1,0:T(8,128)(2,1)} %get-tuple-element.12.gt_a, bf16[3,8,24,128]{3,2,1,0:T(8,128)(2,1)} %get-tuple-element.13.za_a), custom_call_target="tpu_custom_call" | custom-call | tf_op jit(solution)/shard_map/place/pallas_call | solution.py:531

commit v6 on v5

--- a/solution.py
+++ b/solution.py
@@ -213,8 +213,6 @@
     gather_relay(2)
     arrived(ups.at[their_rows], sib_s.at[1], sib_r.at[1])
     arrived(hid.at[their_rows], sib_s.at[0], sib_r.at[0])
-    hid_t[...] = hid[...].T
-    ups_t[...] = ups[...].T
 
     wrapped = jnp.logical_or(z == 0, z == 7)
     allow = jnp.where(wrapped, jnp.where((rows_i >> 6) == (cols_i >> 6), 1.0, 0.0), 1.0).astype(F32)
@@ -368,6 +366,8 @@
 
     gather_end(0)
     project(0)
+    hid_t[...] = hid[...].T
+    ups_t[...] = ups[...].T
     attend(0)
     weight_grads(0)
     sum_start(0)

time: 66.2 us -> 66.2 us (level)
  no operation moved by 1% of the time
where the time goes in v6:
time: 66.2 us; the launch traced here: 66 us
  Pallas kernels  65.4 us (99%)
    pallas_call x1, Pallas kernels, shards(): pl.pallas_call(body, out_shape=shapes[:2] + (pieces,), in_specs=[anywhere...  63.6 us
    pallas_call x1, Pallas kernels, shards(): pl.pallas_call(place_body, out_shape=shapes, in_specs=[anywhere] * 3, out...  1.84 us

profile of v6, /device:TPU:1, one launch (start us, length us, event | category | flops | bytes accessed | tf_op | source)
XLA Modules:
  0.0 66.0 jit_solution(4998272336688245919)
XLA Ops:
  0.6 63.6 %layer.1 = (bf16[128,768]{1,0:T(8,128)(2,1)}, bf16[128,768]{1,0:T(8,128)(2,1)}, bf16[3,8,24,128]{3,2,1,0:T(8,128)(2,1)}) custom-call(bf16[128,768]{1,0:T(8,128)(2,1)} %bitcast.9, bf16[128,768]{1,0:T(8,128)(2,1)} %bitcast.10, bf16[24,2304]{1,0:T(8,128)(2,1)} %wq_hbm.1, bf16[24,768]{1,0:T(8,128)(2,1)} %wp_hbm.1, s32[2,32]{1,0:T(2,128)} %bitcast.11), custom_call_target="tpu_custom_call" | custom-call | tf_op jit(solution)/shard_map/layer/pallas_call | solution.py:520
  64.2 1.8 %place.1 = (bf16[128,768]{1,0:T(8,128)(2,1)}, bf16[128,768]{1,0:T(8,128)(2,1)}, f32[24,2304]{1,0:T(8,128)}, f32[24,768]{1,0:T(8,128)}) custom-call(bf16[128,768]{1,0:T(8,128)(2,1)} %get-tuple-element.11.out_a, bf16[128,768]{1,0:T(8,128)(2,1)} %get-tuple-element.12.gt_a, bf16[3,8,24,128]{3,2,1,0:T(8,128)(2,1)} %get-tuple-element.13.za_a), custom_call_target="tpu_custom_call" | custom-call | tf_op jit(solution)/shard_map/place/pallas_call | solution.py:531
